TPU v7x, 128 devices: a whole 4x4x4 slice. The times are simulated.
128 devices in a mesh: dom: 128 (over x, z, y, core).
Axes of the slice: x: 4, y: 4, z: 4, core: 2. Of those that a mesh axis runs over, the one named last changes fastest.
Arguments:
- features: bfloat16 [262144, 512], P('dom'), may hold values from -6 to 6
- weight: bfloat16 [512, 512], replicated, may hold values from -0.25 to 0.25
- cotangent: bfloat16 [262144, 512], P('dom'), may hold values from -6 to 6
- tile_values: bfloat16 [12288, 128, 128], P('dom'), may hold values from -0.21875 to 0.21875
- tile_rows: int32 [12288], P('dom'), may hold values from 0 to 15
- tile_cols: int32 [12288], P('dom'), may hold values from 0 to 27, as said below
- hub_rows: int32 [512], P('dom'), may hold values from 0 to 2047
- send_rows: int32 [128, 128, 8], P('dom'), may hold values from 0 to 2047
- send_count: int32 [128, 128], P('dom'), may hold values from 1 to 8, as said below
Outputs:
- output: bfloat16 [262144, 512], P('dom')
- grad_features: bfloat16 [262144, 512], P('dom')
- grad_weight: float32 [512, 512], replicated
Inputs may be any that keep to these rules, and one draw needn't show every extreme that they name: `tile_cols`: on every device the first 64 tiles name column blocks below 20 and the other 32 name blocks from 20 on. `send_count`: every source sends 8 rows to at least one device.
All inputs are finite; a program needn't handle non-finite values.
Results may differ from a plain program's by a relative error of at most 0.019.
Values may be sent and summed in bfloat16 or wider, within the bound.
A program may use at most 128 MiB of HBM per device.

v0:
```python
import math

import jax
import jax.numpy as jnp
from jax import lax
from jax.sharding import PartitionSpec as P

LOC_TILES = 64


def one_hot(index, count):
    return (index[:, None] == jnp.arange(count, dtype=jnp.int32)[None, :]).astype(jnp.bfloat16)


def pick_blocks(index, blocks):
    selector = one_hot(index, blocks.shape[0])
    return jnp.einsum("kc,cjf->kjf", selector, blocks, preferred_element_type=jnp.float32).astype(
        blocks.dtype
    )


def add_into(selector, terms):
    upper = terms.astype(jnp.bfloat16)
    lower = (terms - upper.astype(jnp.float32)).astype(jnp.bfloat16)
    first = jnp.einsum("kr,kif->rif", selector, upper, preferred_element_type=jnp.float32)
    return first + jnp.einsum("kr,kif->rif", selector, lower, preferred_element_type=jnp.float32)


def apply_tiles(values, row_idx, col_idx, table_blocks, running):
    tile_count, tile_size = (values.shape[0], values.shape[1])
    group_size = math.gcd(tile_count, 32)
    row_count = running.shape[0]

    def apply_advance(carry, packed):
        vals_group, rows_group, cols_group = packed
        picked = pick_blocks(cols_group, table_blocks)
        products = jnp.einsum(
            "kij,kjf->kif", vals_group, picked, preferred_element_type=jnp.float32
        )
        return (carry + add_into(one_hot(rows_group, row_count), products), None)

    packed = (
        values.reshape(-1, group_size, tile_size, tile_size),
        row_idx.reshape(-1, group_size),
        col_idx.reshape(-1, group_size),
    )
    result, _ = lax.scan(apply_advance, running, packed)
    return result


def spread_tiles(values, row_idx, col_idx, grad_blocks, running):
    tile_count, tile_size = (values.shape[0], values.shape[1])
    group_size = math.gcd(tile_count, 32)
    col_count = running.shape[0]

    def spread_advance(carry, packed):
        vals_group, rows_group, cols_group = packed
        picked = pick_blocks(rows_group, grad_blocks)
        products = jnp.einsum(
            "kij,kif->kjf", vals_group, picked, preferred_element_type=jnp.float32
        )
        return (carry + add_into(one_hot(cols_group, col_count), products), None)

    packed = (
        values.reshape(-1, group_size, tile_size, tile_size),
        row_idx.reshape(-1, group_size),
        col_idx.reshape(-1, group_size),
    )
    result, _ = lax.scan(spread_advance, running, packed)
    return result


def per_device(
    features, weight, cotangent, tile_values, tile_rows, tile_cols, hub_rows, send_rows, send_count
):
    num_dev = lax.axis_size("dom")
    row_count, feat_width = features.shape
    tile_size = tile_values.shape[1]
    row_blocks = row_count // tile_size
    slot_count = send_rows.shape[2]
    split_at = LOC_TILES
    hub_select = one_hot(hub_rows, row_count)
    hub_local = jnp.dot(hub_select, features, preferred_element_type=jnp.float32).astype(
        jnp.bfloat16
    )
    hub_all = lax.all_gather(hub_local, "dom", axis=0, tiled=True)
    targets = send_rows[0]
    counts = send_count[0]
    live_slots = jnp.arange(slot_count, dtype=jnp.int32)[None, :] < counts[:, None]
    target_select = one_hot(targets.reshape(-1), row_count) * live_slots.reshape(-1, 1).astype(
        jnp.bfloat16
    )
    outgoing = (
        jnp.dot(target_select, features, preferred_element_type=jnp.float32)
        .astype(jnp.bfloat16)
        .reshape(num_dev, slot_count, feat_width)
    )
    incoming = lax.all_to_all(outgoing, "dom", split_axis=0, concat_axis=0, tiled=True)
    near_table = jnp.concatenate([features, hub_all], axis=0).reshape(-1, tile_size, feat_width)
    far_table = incoming.reshape(-1, tile_size, feat_width)
    near_blocks = near_table.shape[0]
    empty = jnp.zeros((row_blocks, tile_size, feat_width), jnp.float32)
    summed = apply_tiles(
        tile_values[:split_at], tile_rows[:split_at], tile_cols[:split_at], near_table, empty
    )
    summed = apply_tiles(
        tile_values[split_at:],
        tile_rows[split_at:],
        tile_cols[split_at:] - near_blocks,
        far_table,
        summed,
    )
    aggregated = summed.reshape(row_count, feat_width).astype(jnp.bfloat16)
    pre_act = jnp.dot(aggregated, weight, preferred_element_type=jnp.float32)
    sigmoid_pre = jax.nn.sigmoid(pre_act)
    output = (pre_act * sigmoid_pre).astype(jnp.bfloat16)
    grad_pre = (
        cotangent.astype(jnp.float32) * sigmoid_pre * (1.0 + pre_act * (1.0 - sigmoid_pre))
    ).astype(jnp.bfloat16)
    weight_term = lax.dot_general(
        aggregated, grad_pre, (((0,), (0,)), ((), ())), preferred_element_type=jnp.float32
    )
    weight_term = weight_term * float(row_count * num_dev) ** (-0.5)
    grad_weight = lax.psum(weight_term, "dom")
    grad_agg = lax.dot_general(
        grad_pre, weight, (((1,), (1,)), ((), ())), preferred_element_type=jnp.float32
    ).astype(jnp.bfloat16)
    grad_blocks = grad_agg.reshape(row_blocks, tile_size, feat_width)
    near_grad = spread_tiles(
        tile_values[:split_at],
        tile_rows[:split_at],
        tile_cols[:split_at],
        grad_blocks,
        jnp.zeros((near_blocks, tile_size, feat_width), jnp.float32),
    )
    far_grad = spread_tiles(
        tile_values[split_at:],
        tile_rows[split_at:],
        tile_cols[split_at:] - near_blocks,
        grad_blocks,
        jnp.zeros((far_table.shape[0], tile_size, feat_width), jnp.float32),
    )
    near_flat = near_grad.reshape(-1, feat_width)
    own_grad = near_flat[:row_count]
    hub_grad = near_flat[row_count:]
    far_flat = far_grad.reshape(num_dev, slot_count, feat_width)
    hub_mine = lax.psum_scatter(hub_grad, "dom", scatter_dimension=0, tiled=True)
    returned = lax.all_to_all(
        far_flat.astype(jnp.bfloat16), "dom", split_axis=0, concat_axis=0, tiled=True
    ).astype(far_flat.dtype)
    hub_part = add_into(hub_select, hub_mine[:, None, :])[:, 0, :]
    halo_part = add_into(target_select, returned.reshape(-1, 1, feat_width))[:, 0, :]
    grad_features = own_grad + hub_part + halo_part
    return (output, grad_features.astype(jnp.bfloat16), grad_weight)


def solution(mesh):
    placed = (
        P("dom", None),
        P(),
        P("dom", None),
        P("dom", None, None),
        P("dom"),
        P("dom"),
        P("dom"),
        P("dom", None, None),
        P("dom", None),
    )
    return jax.shard_map(
        per_device,
        mesh=mesh,
        in_specs=placed,
        out_specs=(P("dom", None), P("dom", None), P()),
        check_vma=False,
    )
```

profile of v0, /device:TPU:1, one launch (start us, length us, event | category | flops | bytes accessed | tf_op | source)
XLA Modules:
  0.0 434.4 jit_solution(5442505142722184858)
XLA Ops:
  9.6 4.9 %fusion.69 = bf16[128,8,512]{2,1,0:T(8,128)(2,1)} fusion(bf16[2048,512]{1,0:T(8,128)(2,1)} %param.13, s32[1024]{0:T(1024)S(1)} %eq.165, bf16[1024]{0:T(1024)(128)(2,1)S(1)} %reshape.143), kind=kOutput, calls=%fused_computation.85 | convolution fusion | flops 2152202240 | bytes 3151872 | tf_op jit(solution)/shard_map/dot_general | solution.py:94
  14.5 12.0 %all-to-all-start = ((bf16[128,8,512]{2,1,0:T(8,128)(2,1)}), bf16[128,8,512]{2,1,0:T(8,128)(2,1)}, u32[]{:S(2)}, u32[]{:S(2)}) async-start(bf16[128,8,512]{2,1,0:T(8,128)(2,1)} %fusion.69), calls=%async_computation | async-start | bytes 2097152 | tf_op jit(solution)/shard_map/all_to_all | solution.py:98
  27.1 45.4 %all-gather = bf16[128,4,512]{2,1,0:T(4,128)(2,1)} all-gather(bf16[1,4,512]{2,1,0:T(4,128)(2,1)S(1)} %fusion.72), channel_id=1, replica_groups=mesh['dom'=128] {'dom'}, dimensions={0}, use_global_device_ids=true | all-gather | bytes 528384 | tf_op jit(solution)/shard_map/all_gather | solution.py:86
  73.8 3.1 copy.67
  77.0 42.9 %while.6 = (s32[]{:T(128)}, f32[16,128,512]{2,0,1:T(8,128)}, s32[2,32]{1,0:T(2,128)S(1)}, bf16[2,32,128,128]{3,2,1,0:T(8,128)(2,1)S(1)}, s32[2,32]{1,0:T(2,128)S...) while((s32[]{:T(128)}, f32[16,128,512]{2,0,1:T(8,128)}, s32[2,32]{1,0:T(2,128)S(1)}, ...), condition=%wide.region_1.2_spmd.clone, body=%wide.region_0.1_spmd.clone.sunk | while | flops 768607872 | bytes 45614052 | solution.py:47
  77.0 3.2 convolution_convert_fusion.8
  80.2 4.3 subtract_convert_fusion.8
  84.4 4.8 %fusion.142 = f32[16,128,512]{2,0,1:T(8,128)} fusion(bf16[32,128,512]{2,1,0:T(8,128)(2,1)S(1)} %get-tuple-element.300, s32[32]{0:T(128)S(1)} %get-tuple-element.301), kind=kOutput, calls=%fused_computation.1.clone.1 | convolution fusion | flops 67109376 | bytes 8388736 | tf_op jit(solution)/shard_map/while/body/eval_jaxpr/kr,kif->rif/dot_general | solution.py:26
  89.2 8.6 %select_add_fusion.4 = f32[16,128,512]{2,0,1:T(8,128)} fusion(f32[16,128,512]{2,0,1:T(8,128)} %get-tuple-element.322, f32[16,128,512]{2,0,1:T(8,128)} %fusion.142, bf16[32,128,512]{2,1,0:T(8,128)(2,1)} %get-tuple-element.302, pred[]{:T(512)S(6)} %compare.6, s32[32]{0:T(128)S(1)} %get-tuple-element.301), kind=kOutput, calls=%fused_computation.7.clone.1 | convolution fusion | flops 70255104 | bytes 16777344 | tf_op jit(solution)/shard_map/while/body/eval_jaxpr/kr,kif->rif/dot_general | solution.py:25
  97.9 3.2 convolution_convert_fusion.8
  101.0 4.3 subtract_convert_fusion.8
  105.3 4.8 %fusion.142 = f32[16,128,512]{2,0,1:T(8,128)} fusion(bf16[32,128,512]{2,1,0:T(8,128)(2,1)S(1)} %get-tuple-element.300, s32[32]{0:T(128)S(1)} %get-tuple-element.301), kind=kOutput, calls=%fused_computation.1.clone.1 | convolution fusion | flops 67109376 | bytes 8388736 | tf_op jit(solution)/shard_map/while/body/eval_jaxpr/kr,kif->rif/dot_general | solution.py:26
  110.1 9.8 %select_add_fusion.4 = f32[16,128,512]{2,0,1:T(8,128)} fusion(f32[16,128,512]{2,0,1:T(8,128)} %get-tuple-element.322, f32[16,128,512]{2,0,1:T(8,128)} %fusion.142, bf16[32,128,512]{2,1,0:T(8,128)(2,1)} %get-tuple-element.302, pred[]{:T(512)S(6)} %compare.6, s32[32]{0:T(128)S(1)} %get-tuple-element.301), kind=kOutput, calls=%fused_computation.7.clone.1 | convolution fusion | flops 70255104 | bytes 16777344 | tf_op jit(solution)/shard_map/while/body/eval_jaxpr/kr,kif->rif/dot_general | solution.py:25
  120.0 3.3 copy.65
  123.3 2.7 convolution_convert_fusion.3
  126.0 8.7 %fusion.43 = (bf16[32,128,512]{1,2,0:T(8,128)(2,1)}, bf16[32,128,512]{1,2,0:T(8,128)(2,1)}) fusion(bf16[96,128,128]{2,1,0:T(8,128)(2,1)S(1)} %copy-done.4, bf16[32,128,512]{2,0,1:T(8,128)(2,1)S(1)} %convolution_convert_fusion.3), kind=kOutput, calls=%fused_computation.51 | convolution fusion | flops 545259520 | bytes 13631488 | tf_op jit(solution)/shard_map/while/body/eval_jaxpr/kij,kjf->kif/dot_general | solution.py:37
  134.7 8.0 %copy.71 = bf16[32,128,512]{2,0,1:T(8,128)(2,1)} copy(bf16[32,128,512]{1,2,0:T(8,128)(2,1)} %get-tuple-element.216) | data formatting | bytes 8388608 | tf_op jit(solution)/shard_map/while/body/eval_jaxpr/convert_element_type | solution.py:23
  142.7 7.9 %copy.72 = bf16[32,128,512]{2,0,1:T(8,128)(2,1)} copy(bf16[32,128,512]{1,2,0:T(8,128)(2,1)} %get-tuple-element.215) | data formatting | bytes 8388608 | tf_op jit(solution)/shard_map/while/body/eval_jaxpr/convert_element_type | solution.py:24
  150.6 3.0 fusion.86
  154.1 1.3 copy-done.7
  158.0 3.8 multiply_convert_fusion
  161.8 1.3 convolution_convert_fusion.2
  163.1 1.2 copy.74
  164.3 1.5 convolution_convert_fusion.4
  166.2 8.8 %fusion.42 = (bf16[32,128,512]{1,2,0:T(8,128)(2,1)}, bf16[32,128,512]{1,2,0:T(8,128)(2,1)}) fusion(bf16[96,128,128]{2,1,0:T(8,128)(2,1)S(1)} %copy-done.5, bf16[32,128,512]{2,0,1:T(8,128)(2,1)S(1)} %convolution_convert_fusion.4), kind=kOutput, calls=%fused_computation.48 | convolution fusion | flops 545259520 | bytes 13631488 | tf_op jit(solution)/shard_map/while/body/eval_jaxpr/kij,kif->kjf/dot_general | solution.py:59
  175.0 7.9 %copy.79 = bf16[32,128,512]{2,0,1:T(8,128)(2,1)} copy(bf16[32,128,512]{1,2,0:T(8,128)(2,1)} %get-tuple-element.214) | data formatting | bytes 8388608 | tf_op jit(solution)/shard_map/while/body/eval_jaxpr/convert_element_type | solution.py:23
  183.0 4.1 fusion.93
  187.1 7.9 %copy.80 = bf16[32,128,512]{2,0,1:T(8,128)(2,1)} copy(bf16[32,128,512]{1,2,0:T(8,128)(2,1)} %get-tuple-element.213) | data formatting | bytes 8388608 | tf_op jit(solution)/shard_map/while/body/eval_jaxpr/convert_element_type | solution.py:24
  195.0 3.5 add_convert_fusion.1
  198.6 1.3 copy.81
  199.9 4.9 %all-to-all-start.1 = ((bf16[128,8,512]{2,1,0:T(8,128)(2,1)}), bf16[128,8,512]{2,1,0:T(8,128)(2,1)}, u32[]{:S(2)}, u32[]{:S(2)}) async-start(bf16[128,8,512]{2,1,0:T(8,128)(2,1)} %bitcast.126), calls=%async_computation.1 | async-start | bytes 2097152 | tf_op jit(solution)/shard_map/all_to_all | solution.py:148
  204.8 46.0 %while.7 = (s32[]{:T(128)}, f32[20,128,512]{2,0,1:T(8,128)}, s32[2,32]{1,0:T(2,128)S(1)}, bf16[2,32,128,128]{2,3,1,0:T(8,128)(2,1)}, s32[2,32]{1,0:T(2,128)S(1)}...) while((s32[]{:T(128)}, f32[20,128,512]{2,0,1:T(8,128)}, s32[2,32]{1,0:T(2,128)S(1)}, ...), condition=%wide.region_3.4_spmd.clone, body=%wide.region_2.3_spmd.clone.sunk | while | flops 786171648 | bytes 57672704 | solution.py:69
  204.9 1.3 convolution_convert_fusion.9
  206.4 4.2 subtract_convert_fusion.9
  210.6 5.8 %fusion.150 = f32[20,128,512]{2,0,1:T(8,128)} fusion(bf16[32,128,512]{2,1,0:T(8,128)(2,1)S(1)} %get-tuple-element.310, s32[32]{0:T(128)S(1)} %get-tuple-element.311), kind=kOutput, calls=%fused_computation.25.clone.1 | convolution fusion | flops 83886720 | bytes 9437312 | tf_op jit(solution)/shard_map/while/body/eval_jaxpr/kr,kif->rif/dot_general | solution.py:26
  216.4 10.4 %select_add_fusion.5 = f32[20,128,512]{2,0,1:T(8,128)} fusion(f32[20,128,512]{2,0,1:T(8,128)} %get-tuple-element.346, f32[20,128,512]{2,0,1:T(8,128)} %fusion.150, pred[]{:T(512)S(6)} %compare.7, bf16[32,128,512]{2,1,0:T(8,128)(2,1)} %get-tuple-element.312, s32[32]{0:T(128)S(1)} %get-tuple-element.311), kind=kOutput, calls=%fused_computation.24.clone.1 | convolution fusion | flops 87818880 | bytes 19923072 | tf_op jit(solution)/shard_map/while/body/eval_jaxpr/kr,kif->rif/dot_general | solution.py:25
  226.8 1.3 convolution_convert_fusion.9
  228.4 4.2 subtract_convert_fusion.9
  232.6 5.8 %fusion.150 = f32[20,128,512]{2,0,1:T(8,128)} fusion(bf16[32,128,512]{2,1,0:T(8,128)(2,1)S(1)} %get-tuple-element.310, s32[32]{0:T(128)S(1)} %get-tuple-element.311), kind=kOutput, calls=%fused_computation.25.clone.1 | convolution fusion | flops 83886720 | bytes 9437312 | tf_op jit(solution)/shard_map/while/body/eval_jaxpr/kr,kif->rif/dot_general | solution.py:26
  238.4 12.2 %select_add_fusion.5 = f32[20,128,512]{2,0,1:T(8,128)} fusion(f32[20,128,512]{2,0,1:T(8,128)} %get-tuple-element.346, f32[20,128,512]{2,0,1:T(8,128)} %fusion.150, pred[]{:T(512)S(6)} %compare.7, bf16[32,128,512]{2,1,0:T(8,128)(2,1)} %get-tuple-element.312, s32[32]{0:T(128)S(1)} %get-tuple-element.311), kind=kOutput, calls=%fused_computation.24.clone.1 | convolution fusion | flops 87818880 | bytes 19923072 | tf_op jit(solution)/shard_map/while/body/eval_jaxpr/kr,kif->rif/dot_general | solution.py:25
  250.8 6.0 %copy.76 = f32[20,128,512]{2,1,0:T(8,128)S(1)} copy(f32[20,128,512]{2,0,1:T(8,128)} %get-tuple-element.104) | data formatting | bytes 10485760 | tf_op jit(solution)/shard_map/while | solution.py:69
  258.3 4.4 %copy.75 = f32[16,128,512]{2,1,0:T(8,128)} copy(f32[16,128,512]{2,0,1:T(8,128)S(1)} %slice.58) | data formatting | bytes 8388608 | tf_op jit(solution)/shard_map/slice | solution.py:144
  262.7 2.3 convolution_multiply_fusion
  265.0 5.7 %fusion.47 = f32[2048,512]{1,0:T(8,128)} fusion(s32[1024]{0:T(1024)S(1)} %copy-done.16, bf16[1024]{0:T(1024)(128)(2,1)S(1)} %copy-done.18, bf16[128,8,512]{2,1,0:T(8,128)(2,1)} %all-to-all-done.1), kind=kOutput, calls=%fused_computation.55 | convolution fusion | flops 2151677952 | bytes 5249024 | tf_op jit(solution)/shard_map/kr,kif->rif/dot_general | solution.py:25
  270.8 5.8 %fusion.45 = f32[2048,512]{1,0:T(8,128)} fusion(s32[1024]{0:T(1024)S(1)} %copy-done.16, bf16[1024]{0:T(1024)(128)(2,1)S(1)} %copy-done.18, bf16[128,8,512]{2,1,0:T(8,128)(2,1)} %all-to-all-done.1), kind=kOutput, calls=%fused_computation.54 | convolution fusion | flops 2153250816 | bytes 5249024 | tf_op jit(solution)/shard_map/kr,kif->rif/dot_general | solution.py:26
  276.5 140.7 %all-reduce.4.cloned.1.call-done = (f32[512,512]{1,0:T(8,128)}, f32[512,512]{1,0:T(8,128)}) async-done(((f32[512,512]{1,0:T(8,128)}, f32[512,512]{1,0:T(8,128)}), (f32[512,512]{1,0:T(8,128)}, f32[512,512]{1,0:T(8,128)})) %all-reduce.4.cloned.1.call-update) | async-done | bytes 2097168
  417.3 1.7 fusion.79
  419.5 6.6 %fusion.52 = bf16[2048,512]{1,0:T(8,128)(2,1)} fusion(f32[16,128,512]{2,1,0:T(8,128)S(1)} %copy-done.8, f32[2048,512]{1,0:T(8,128)} %fusion.47, f32[2048,512]{1,0:T(8,128)} %fusion.45, f32[2048,512]{1,0:T(8,128)S(1)} %fusion.79, s32[4]{0:T(128)S(1)} %copy-done.14, f32[512,512]{1,0:T(8,128)} %get-tuple-element.207, u32[]{:T(128)S(6)} %multiply.1), kind=kOutput, calls=%fused_computation.59 | convolution fusion | flops 13647872 | bytes 18882580 | tf_op jit(solution)/shard_map/kr,kif->rif/dot_general | solution.py:26
  (77 shorter events, 11.5 us)
Async XLA Ops:
  7.2 150.4 %copy-start = (bf16[512,512]{1,0:T(8,128)(2,1)S(1)}, bf16[512,512]{1,0:T(8,128)(2,1)}, u32[]{:S(2)}) copy-start(bf16[512,512]{1,0:T(8,128)(2,1)} %param.14) | copy-start | bytes 1572868
  8.1 0.9 copy-start.15
  9.0 0.6 copy-start.17
  14.5 12.0 %copy-start.20 = (s32[96]{0:T(128)S(1)}, s32[96]{0:T(128)}, u32[]{:S(2)}) copy-start(s32[96]{0:T(128)} %param.17) | copy-start | bytes 1156
  14.5 12.1 %copy-start.21 = (s32[96]{0:T(128)S(1)}, s32[96]{0:T(128)}, u32[]{:S(2)}) copy-start(s32[96]{0:T(128)} %param.18) | copy-start | bytes 1156
  14.5 12.2 %copy-start.9 = (bf16[2048,512]{1,0:T(8,128)(2,1)S(1)}, bf16[2048,512]{1,0:T(8,128)(2,1)}, u32[]{:S(2)}) copy-start(bf16[2048,512]{1,0:T(8,128)(2,1)} %param.13) | copy-start | bytes 6291460
  14.5 12.2 %copy-start.13 = (s32[4]{0:T(128)S(1)}, s32[4]{0:T(128)}, u32[]{:S(2)}) copy-start(s32[4]{0:T(128)} %param.19) | copy-start | bytes 52
  14.5 108.8 %all-to-all-start = ((bf16[128,8,512]{2,1,0:T(8,128)(2,1)}), bf16[128,8,512]{2,1,0:T(8,128)(2,1)}, u32[]{:S(2)}, u32[]{:S(2)}) async-start(bf16[128,8,512]{2,1,0:T(8,128)(2,1)} %fusion.69), calls=%async_computation | async-start | bytes 2097152 | tf_op jit(solution)/shard_map/all_to_all | solution.py:98
  73.8 3.2 slice-start
  123.3 2.7 copy-start.4
  150.6 3.4 copy-start.3
  150.6 4.7 %copy-start.7 = (bf16[32,128,512]{2,0,1:T(8,128)(2,1)S(1)}, bf16[32,128,512]{2,0,1:T(8,128)(2,1)}, u32[]{:S(2)}) copy-start(bf16[32,128,512]{2,0,1:T(8,128)(2,1)} %copy.72) | copy-start | bytes 12582916
  156.4 1.6 copy-start.19
  157.6 4.2 copy-start.10
  161.8 1.3 copy-start.22
  164.3 1.9 copy-start.5
  199.9 65.1 %all-to-all-start.1 = ((bf16[128,8,512]{2,1,0:T(8,128)(2,1)}), bf16[128,8,512]{2,1,0:T(8,128)(2,1)}, u32[]{:S(2)}, u32[]{:S(2)}) async-start(bf16[128,8,512]{2,1,0:T(8,128)(2,1)} %bitcast.126), calls=%async_computation.1 | async-start | bytes 2097152 | tf_op jit(solution)/shard_map/all_to_all | solution.py:148
  204.8 212.5 %all-reduce.4.cloned.1.call-start = ((), (), s32[]{:S(2)}) async-start(), calls=%async_computation.2 | async-start | bytes 4194304
  204.8 1.6 copy-start.6
  226.8 1.6 copy-start.6
  250.8 6.0 %copy-start.2 = (f32[20,128,512]{2,0,1:T(8,128)S(1)}, f32[20,128,512]{2,0,1:T(8,128)}, u32[]{:S(2)}) copy-start(f32[20,128,512]{2,0,1:T(8,128)} %get-tuple-element.104) | copy-start | bytes 15728644
  258.3 4.4 %copy-start.11 = (bf16[16,128,512]{2,1,0:T(8,128)(2,1)S(1)}, bf16[16,128,512]{2,1,0:T(8,128)(2,1)}, u32[]{:S(2)}) copy-start(bf16[16,128,512]{2,1,0:T(8,128)(2,1)} %copy-done.10) | copy-start | bytes 6291460
  258.3 4.4 %copy-start.23 = (bf16[2048,512]{1,0:T(8,128)(2,1)S(1)}, bf16[2048,512]{1,0:T(8,128)(2,1)}, u32[]{:S(2)}) copy-start(bf16[2048,512]{1,0:T(8,128)(2,1)} %copy-done.22) | copy-start | bytes 6291460
  262.7 2.3 copy-start.16
  262.7 2.3 copy-start.18
  270.8 146.5 %copy-start.14 = (s32[4]{0:T(128)S(1)}, s32[4]{0:T(128)}, u32[]{:S(2)}) copy-start(s32[4]{0:T(128)} %param.19) | copy-start | bytes 52
  417.3 2.2 copy-start.8
  419.5 6.6 %copy-start.12 = (f32[512,512]{1,0:T(8,128)S(1)}, f32[512,512]{1,0:T(8,128)}, u32[]{:S(2)}) copy-start(f32[512,512]{1,0:T(8,128)} %get-tuple-element.363) | copy-start | bytes 3145732
  419.5 7.6 %copy-start.1 = (bf16[512,512]{1,0:T(8,128)(2,1)S(1)}, bf16[512,512]{1,0:T(8,128)(2,1)}, u32[]{:S(2)}) copy-start(bf16[512,512]{1,0:T(8,128)(2,1)} %param.14) | copy-start | bytes 1572868
Sparse Core Ops, SparseCore 0:
  265.1 152.1 all-reduce.3
where the time goes:
time: 438 us; the launch traced here: 434 us
  matrix products  154 us (35%)
  waiting for transfers between devices  141 us (32%)
  local copies, waits for them, and re-layouts  61.2 us (14%)
  blocking collectives  45.4 us (10%)
  starting transfers between devices  16.9 us (4%)
  between operations  14.8 us (3%)
    unnamed x2, waiting for transfers between devices  141 us
    dot_general x8, matrix products, add_into(): jnp.einsum('kr,kif->rif', selector, upper, preferred_element_type=jnp.flo...  55.5 us
    all_gather x1, blocking collectives, per_device(): hub_all = lax.all_gather(hub_local, 'dom', axis=0, tiled=True)  45.4 us
    dot_general x8, matrix products, add_into(): jnp.einsum('kr,kif->rif', selector, lower, preferred_element_type=jnp.flo...  38.1 us
    dot_general x3, matrix products, spread_advance(): jnp.einsum('kij,kif->kjf', vals_group, picked, preferred_element_type=jnp...  17.3 us
    dot_general x3, matrix products, apply_advance(): jnp.einsum('kij,kjf->kif', vals_group, picked, preferred_element_type=jnp...  17.2 us
    convert_element_type x2, local copies, waits for them, and re-layouts, add_into(): upper = terms.astype(jnp.bfloat16)  15.9 us
    convert_element_type x2, local copies, waits for them, and re-layouts, add_into(): lower = (terms - upper.astype(jnp.float32)).astype(jnp.bfloat16)  15.9 us
  transfers between devices with their start and end apart: 3, of which 1 were waited for; matrix products, arithmetic and copies ran while one was open for 28% of the time, Pallas kernels for 0%

commit v1 on v0

v1 whole, which is shorter than its diff:
```python
import functools

import jax
import jax.numpy as jnp
from jax import lax
from jax.experimental import pallas as pl
from jax.experimental.pallas import tpu as pltpu
from jax.sharding import PartitionSpec as P

MESH = pl.DeviceIdType.MESH
N = 128
F = 512
R = 2048
TILE = 128
SLOTS = 8
HUBS = 4
TILES = 96
F32 = jnp.float32
BF16 = jnp.bfloat16
VMEM_SPEC = pl.BlockSpec(memory_space=pltpu.VMEM)
ANY_SPEC = pl.BlockSpec(memory_space=pl.ANY)
SMEM_SPEC = pl.BlockSpec(memory_space=pltpu.SMEM)
LIMIT = 60 * 1024 * 1024


def peer_of(me, i):
    return lax.rem(me + i, N)


def greet():
    me = lax.axis_index("dom")
    barrier = pltpu.get_barrier_semaphore()

    @pl.loop(1, N)
    def _(i):
        pl.semaphore_signal(barrier, inc=1, device_id=(peer_of(me, i),), device_id_type=MESH)

    return barrier


def meet(barrier):
    pl.semaphore_wait(barrier, N - 1)


def whole_wait(ref, sem):
    pltpu.make_async_copy(ref, ref, sem).wait()


def halo_send(idx_ref, hub_idx_ref, feat_ref, far_ref, hub_ref, out_buf, hub_buf, send, recv):
    me = lax.axis_index("dom")
    barrier = greet()
    feats = feat_ref[...]
    lanes = lax.broadcasted_iota(jnp.int32, (TILE, R), 1)
    for b in range(N * SLOTS // TILE):
        picks = (idx_ref[pl.ds(b * TILE, TILE), :] == lanes).astype(F32).astype(BF16)
        rows = jnp.dot(picks, feats, preferred_element_type=F32)
        out_buf[pl.ds(b * 16, 16)] = rows.reshape(16, SLOTS, F).astype(BF16)
    picks = (hub_idx_ref[...] == lanes[:8]).astype(F32).astype(BF16)
    rows = jnp.dot(picks, feats, preferred_element_type=F32)
    hub_buf[0] = rows[:HUBS].astype(BF16)
    meet(barrier)
    own = (
        pltpu.make_async_copy(out_buf.at[me], far_ref.at[me], recv.at[0]),
        pltpu.make_async_copy(hub_buf.at[0], hub_ref.at[me], recv.at[1]),
    )
    for copy in own:
        copy.start()

    @pl.loop(1, N)
    def _(i):
        peer = peer_of(me, i)
        pltpu.make_async_remote_copy(
            src_ref=out_buf.at[peer], dst_ref=far_ref.at[me], send_sem=send.at[0],
            recv_sem=recv.at[0], device_id=(peer,), device_id_type=MESH,
        ).start()
        pltpu.make_async_remote_copy(
            src_ref=hub_buf.at[0], dst_ref=hub_ref.at[me], send_sem=send.at[1],
            recv_sem=recv.at[1], device_id=(peer,), device_id_type=MESH,
        ).start()

    whole_wait(out_buf.at[pl.ds(0, N - 1)], send.at[0])
    whole_wait(hub_ref.at[pl.ds(0, N - 1)], send.at[1])
    whole_wait(far_ref, recv.at[0])
    whole_wait(hub_ref, recv.at[1])


def call_halo_send(idx, hub_idx, features):
    return pl.pallas_call(
        halo_send,
        out_shape=(
            jax.ShapeDtypeStruct((N, SLOTS, F), BF16),
            jax.ShapeDtypeStruct((N, HUBS, F), BF16),
        ),
        in_specs=[VMEM_SPEC] * 3,
        out_specs=(ANY_SPEC, ANY_SPEC),
        scratch_shapes=[
            pltpu.VMEM((N, SLOTS, F), BF16),
            pltpu.VMEM((1, HUBS, F), BF16),
            pltpu.SemaphoreType.DMA((2,)),
            pltpu.SemaphoreType.DMA((2,)),
        ],
        compiler_params=pltpu.CompilerParams(
            collective_id=0, has_side_effects=True, vmem_limit_bytes=LIMIT
        ),
        name="halo_send",
    )(idx, hub_idx, features)


def layer(
    rows_ref, cols_ref, tiles_ref, feat_ref, hub_ref, far_ref, cot_ref, weight_ref,
    out_ref, own_ref, hub_grad_ref, far_grad_ref, term_ref,
    tiles, table, cot, acc, grads, gagg, term, sems,
):
    loads = (
        pltpu.make_async_copy(tiles_ref, tiles, sems.at[0]),
        pltpu.make_async_copy(feat_ref, table.at[pl.ds(0, 16)], sems.at[1]),
        pltpu.make_async_copy(hub_ref, table.at[pl.ds(16, 4)], sems.at[2]),
        pltpu.make_async_copy(far_ref, table.at[pl.ds(20, 8)], sems.at[3]),
        pltpu.make_async_copy(cot_ref, cot, sems.at[4]),
    )
    for copy in loads:
        copy.start()
    acc[...] = jnp.zeros_like(acc)
    for copy in loads[:4]:
        copy.wait()

    @pl.loop(0, TILES // 4)
    def _(k):
        for u in range(4):
            t = 4 * k + u
            acc[rows_ref[t]] += jnp.dot(
                tiles[t], table[cols_ref[t]], preferred_element_type=F32
            )

    loads[4].wait()
    term[...] = jnp.zeros_like(term)
    weight = weight_ref[...]

    @pl.loop(0, 8)
    def _(k):
        agg = acc[pl.ds(2 * k, 2)].reshape(256, F).astype(BF16)
        pre = jnp.dot(agg, weight, preferred_element_type=F32)
        sig = 0.5 * jnp.tanh(0.5 * pre) + 0.5
        here = pl.ds(pl.multiple_of(k * 256, 256), 256)
        out_ref[here, :] = (pre * sig).astype(BF16)
        gpre = (cot[here, :].astype(F32) * sig * (1.0 + pre * (1.0 - sig))).astype(BF16)
        term[...] += lax.dot_general(
            agg, gpre, (((0,), (0,)), ((), ())), preferred_element_type=F32
        )
        back = lax.dot_general(gpre, weight, (((1,), (1,)), ((), ())), preferred_element_type=F32)
        gagg[pl.ds(2 * k, 2)] = back.astype(BF16).reshape(2, TILE, F)

    term_ref[...] = (term[...] * (1.0 / 512.0)).astype(BF16)
    grads[...] = jnp.zeros_like(grads)

    @pl.loop(0, TILES // 4)
    def _(k):
        for u in range(4):
            t = 4 * k + u
            grads[cols_ref[t]] += lax.dot_general(
                tiles[t], gagg[rows_ref[t]], (((0,), (0,)), ((), ())), preferred_element_type=F32
            )

    own_ref[...] = grads[pl.ds(0, 16)]
    hub_grad_ref[...] = grads[pl.ds(16, 4)].astype(BF16)
    far_grad_ref[...] = grads[pl.ds(20, 8)].astype(BF16)


def call_layer(rows, cols, tiles, feats, hubs, far, cot, weight):
    return pl.pallas_call(
        layer,
        out_shape=(
            jax.ShapeDtypeStruct((R, F), BF16),
            jax.ShapeDtypeStruct((16, TILE, F), F32),
            jax.ShapeDtypeStruct((4, TILE, F), BF16),
            jax.ShapeDtypeStruct((8, TILE, F), BF16),
            jax.ShapeDtypeStruct((F, F), BF16),
        ),
        in_specs=[SMEM_SPEC] * 2 + [ANY_SPEC] * 5 + [VMEM_SPEC],
        out_specs=(VMEM_SPEC,) * 5,
        scratch_shapes=[
            pltpu.VMEM((TILES, TILE, TILE), BF16),
            pltpu.VMEM((28, TILE, F), BF16),
            pltpu.VMEM((R, F), BF16),
            pltpu.VMEM((16, TILE, F), F32),
            pltpu.VMEM((28, TILE, F), F32),
            pltpu.VMEM((16, TILE, F), BF16),
            pltpu.VMEM((F, F), F32),
            pltpu.SemaphoreType.DMA((5,)),
        ],
        compiler_params=pltpu.CompilerParams(vmem_limit_bytes=LIMIT),
        name="layer",
    )(rows, cols, tiles, feats, hubs, far, cot, weight)


def grad_return(
    idx_ref, hub_idx_ref, far_ref, hub_ref, term_ref, own_ref,
    out_ref, weight_ref,
    far_in, hub_in, term_in, share, gathered, picks, send, recv,
):
    me = lax.axis_index("dom")
    barrier = greet()
    rows = lax.broadcasted_iota(jnp.int32, (TILE, N * SLOTS), 0)

    @pl.loop(0, 16)
    def _(k):
        here = pl.ds(pl.multiple_of(k * TILE, TILE), TILE)
        picks[here, :] = (idx_ref[...] == rows + k * TILE).astype(F32).astype(BF16)

    meet(barrier)
    pltpu.make_async_copy(term_ref.at[me], term_in.at[me], recv.at[0]).start()
    pltpu.make_async_copy(hub_ref.at[me], hub_in.at[me], recv.at[1]).start()
    pltpu.make_async_copy(far_ref.at[me], far_in.at[me], recv.at[2]).start()

    for s, (src, dst) in enumerate(((term_ref, term_in), (hub_ref, hub_in), (far_ref, far_in))):
        @pl.loop(1, N)
        def _(i):
            peer = peer_of(me, i)
            pltpu.make_async_remote_copy(
                src_ref=src.at[peer], dst_ref=dst.at[me], send_sem=send.at[s],
                recv_sem=recv.at[s], device_id=(peer,), device_id_type=MESH,
            ).start()

    whole_wait(term_in, recv.at[0])
    share[0] = jnp.sum(term_in[...].astype(F32), axis=0).astype(BF16)
    pltpu.make_async_copy(share.at[0], gathered.at[me], recv.at[3]).start()

    @pl.loop(1, N)
    def _(i):
        peer = peer_of(me, i)
        pltpu.make_async_remote_copy(
            src_ref=share.at[0], dst_ref=gathered.at[me], send_sem=send.at[3],
            recv_sem=recv.at[3], device_id=(peer,), device_id_type=MESH,
        ).start()

    whole_wait(hub_in, recv.at[1])
    hub_sum = jnp.sum(hub_in[...].astype(F32), axis=0)
    whole_wait(far_in, recv.at[2])
    returned = far_in[...].reshape(N * SLOTS, F)

    lane_rows = lax.broadcasted_iota(jnp.int32, (TILE, F), 0)

    @pl.loop(0, 16)
    def _(k):
        here = pl.ds(pl.multiple_of(k * TILE, TILE), TILE)
        total = own_ref[here, :] + jnp.dot(picks[here, :], returned, preferred_element_type=F32)
        for j in range(HUBS):
            mine = lane_rows + k * TILE == hub_idx_ref[j]
            total += jnp.where(mine, hub_sum[j : j + 1, :], 0.0)
        out_ref[here, :] = total.astype(BF16)

    whole_wait(gathered, recv.at[3])
    weight_ref[...] = gathered[...].astype(F32)
    for s, ref in enumerate((term_in, hub_in, far_in, gathered)):
        whole_wait(ref.at[pl.ds(0, N - 1)], send.at[s])


def call_grad_return(idx, hub_idx, far, hub, term, own):
    return pl.pallas_call(
        grad_return,
        out_shape=(
            jax.ShapeDtypeStruct((R, F), BF16),
            jax.ShapeDtypeStruct((N, 4, F), F32),
        ),
        in_specs=[VMEM_SPEC, SMEM_SPEC] + [VMEM_SPEC] * 4,
        out_specs=(VMEM_SPEC, VMEM_SPEC),
        scratch_shapes=[
            pltpu.VMEM((N, SLOTS, F), BF16),
            pltpu.VMEM((N, HUBS, F), BF16),
            pltpu.VMEM((N, 4, F), BF16),
            pltpu.VMEM((1, 4, F), BF16),
            pltpu.VMEM((N, 4, F), BF16),
            pltpu.VMEM((R, N * SLOTS), BF16),
            pltpu.SemaphoreType.DMA((4,)),
            pltpu.SemaphoreType.DMA((4,)),
        ],
        compiler_params=pltpu.CompilerParams(
            collective_id=1, has_side_effects=True, vmem_limit_bytes=LIMIT
        ),
        name="grad_return",
    )(idx, hub_idx, far, hub, term, own)


def per_device(
    features, weight, cotangent, tile_values, tile_rows, tile_cols, hub_rows, send_rows, send_count
):
    live = jnp.arange(SLOTS, dtype=jnp.int32)[None, :] < send_count[0][:, None]
    idx = jnp.where(live, send_rows[0], -1)
    hub_col = jnp.concatenate([hub_rows, jnp.full((4,), -1, jnp.int32)]).reshape(8, 1)
    far, hub = call_halo_send(idx.reshape(N * SLOTS, 1), hub_col, features)
    output, own, hub_grad, far_grad, term = call_layer(
        tile_rows, tile_cols, tile_values, features.reshape(16, TILE, F),
        hub.reshape(4, TILE, F), far.reshape(8, TILE, F), cotangent, weight,
    )
    grad_features, grad_weight = call_grad_return(
        idx.reshape(1, N * SLOTS), hub_rows, far_grad.reshape(N, SLOTS, F),
        hub_grad.reshape(N, HUBS, F), term.reshape(N, 4, F), own.reshape(R, F),
    )
    return output, grad_features, grad_weight.reshape(F, F)


def solution(mesh):
    placed = (
        P("dom", None),
        P(),
        P("dom", None),
        P("dom", None, None),
        P("dom"),
        P("dom"),
        P("dom"),
        P("dom", None, None),
        P("dom", None),
    )
    return jax.shard_map(
        per_device,
        mesh=mesh,
        in_specs=placed,
        out_specs=(P("dom", None), P("dom", None), P()),
        check_vma=False,
    )
```

time: 438 us -> 134 us (0.31)
  matrix products: 154 us -> 0 us
  waiting for transfers between devices: 141 us -> 0 us
  Pallas kernels: 0 us -> 118 us
  local copies, waits for them, and re-layouts: 61.2 us -> 12.6 us
  blocking collectives: 45.4 us -> 0 us
  starting transfers between devices: 16.9 us -> 0 us
  between operations: 14.8 us -> 0.69 us
    dot_general x33 -> x0, matrix products: 154 us -> none  [the longest x8 55.5 us: add_into(): jnp.einsum('kr,kif->rif', selector, upper, preferred_element_type=jnp.flo...]
    unnamed x2 -> x0, waiting for transfers between devices: 141 us -> none
    pallas_call x0 -> x3, Pallas kernels: none -> 118 us  [the longest x1 52.3 us: call_grad_return(): pl.pallas_call(grad_return, out_shape=(jax.ShapeDtypeStruct((R, F), BF16)...]
    all_gather x1 -> x0, blocking collectives: 45.4 us -> none  [per_device(): hub_all = lax.all_gather(hub_local, 'dom', axis=0, tiled=True)]
    convert_element_type x7 -> x0, local copies, waits for them, and re-layouts: 34.3 us -> none  [the longest x2 15.9 us: add_into(): upper = terms.astype(jnp.bfloat16)]
    all_to_all x2 -> x0, starting transfers between devices: 16.9 us -> none  [the longest x1 12 us: per_device(): lax.all_to_all(outgoing, 'dom', split_axis=0, concat_axis=0, tiled=True)]
    reshape x2 -> x6, local copies, waits for them, and re-layouts: 0.16 us -> 9.91 us  [the longest x1 2.7 us: per_device(): return (output, grad_features, grad_weight.reshape(F, F))]
    slice x7 -> x0, local copies, waits for them, and re-layouts: 9.22 us -> none  [the longest x2 4.85 us: per_device(): own_grad = near_flat[:row_count]]
  transfers between devices with their start and end apart: 3 -> 0, of which waited for: 1 -> 0; matrix products, arithmetic and copies ran while one was open for 28% -> 0% of each run, Pallas kernels for 0% -> 0%
where the time goes in v1:
time: 134 us; the launch traced here: 133 us
  Pallas kernels  118 us (88%)
  local copies, waits for them, and re-layouts  12.6 us (9%)
  other arithmetic  2.19 us (2%)
    pallas_call x1, Pallas kernels, call_grad_return(): pl.pallas_call(grad_return, out_shape=(jax.ShapeDtypeStruct((R, F), BF16)...  52.3 us
    pallas_call x1, Pallas kernels, call_halo_send(): pl.pallas_call(halo_send, out_shape=(jax.ShapeDtypeStruct((N, SLOTS, F),...  36.1 us
    pallas_call x1, Pallas kernels, call_layer(): pl.pallas_call(layer, out_shape=(jax.ShapeDtypeStruct((R, F), BF16), jax....  29.2 us
    reshape x1, local copies, waits for them, and re-layouts, per_device(): return (output, grad_features, grad_weight.reshape(F, F))  2.7 us

profile of v1, /device:TPU:1, one launch (start us, length us, event | category | flops | bytes accessed | tf_op | source)
XLA Modules:
  0.0 133.1 jit_solution(6448138131892843029)
XLA Ops:
  0.6 0.7 pad_bitcast_fusion
  1.3 0.7 copy.18.hub_idx_ref
  2.0 0.7 iota_compare_fusion
  2.7 0.1 lt.40
  2.8 0.8 copy.15
  3.6 0.1 squeeze.6
  3.7 0.6 broadcast_select_fusion.1.idx_ref
  4.3 0.2 lt.41
  4.5 0.2 squeeze.7
  4.7 0.8 broadcast_select_fusion.idx_ref
  5.6 36.1 %halo_send.1 = (bf16[128,8,512]{2,1,0:T(8,128)(2,1)}, bf16[128,4,512]{2,1,0:T(4,128)(2,1)}) custom-call(s32[1024,1]{1,0:T(8,128)} %broadcast_select_fusion.idx_ref, s32[8,1]{1,0:T(8,128)} %copy.18.hub_idx_ref, bf16[2048,512]{1,0:T(8,128)(2,1)} %feat_ref.1), custom_call_target="tpu_custom_call" | custom-call | tf_op jit(solution)/shard_map/halo_send/pallas_call | solution.py:88
  41.7 2.0 %reshape.102.hub_ref = bf16[4,128,512]{2,1,0:T(8,128)(2,1)} reshape(bf16[128,4,512]{2,1,0:T(4,128)(2,1)} %get-tuple-element.12) | data formatting | bytes 1048576 | tf_op jit(solution)/shard_map/reshape | solution.py:293
  43.7 29.2 %layer.1 = (bf16[2048,512]{1,0:T(8,128)(2,1)}, f32[16,128,512]{2,1,0:T(8,128)}, bf16[4,128,512]{2,1,0:T(8,128)(2,1)}, bf16[8,128,512]{2,1,0:T(8,128)(2,1)}, bf16[512,512]{1,0:T(8,128)(2,1)}) custom-call(s32[96]{0:T(128)} %rows_ref.1, s32[96]{0:T(128)} %cols_ref.1, bf16[96,128,128]{2,1,0:T(8,128)(2,1)} %tiles_ref.1, bf16[16,128,512]{2,1,0:T(8,128)(2,1)} %bitcast.7, ...), custom_call_target="tpu_custom_call" | custom-call | tf_op jit(solution)/shard_map/layer/pallas_call | solution.py:170
  72.9 2.0 %reshape.105.hub_ref = bf16[128,4,512]{2,1,0:T(4,128)(2,1)} reshape(bf16[4,128,512]{2,1,0:T(8,128)(2,1)} %get-tuple-element.16) | data formatting | bytes 1048576 | tf_op jit(solution)/shard_map/reshape | solution.py:297
  74.9 1.9 %reshape.106.term_ref = bf16[128,4,512]{2,1,0:T(4,128)(2,1)} reshape(bf16[512,512]{1,0:T(8,128)(2,1)} %get-tuple-element.17) | data formatting | bytes 1048576 | tf_op jit(solution)/shard_map/reshape | solution.py:297
  76.8 52.3 %grad_return.1 = (bf16[2048,512]{1,0:T(8,128)(2,1)}, f32[128,4,512]{2,1,0:T(4,128)}) custom-call(s32[1,1024]{1,0:T(1,128)} %broadcast_select_fusion.1.idx_ref, s32[4]{0:T(128)} %hub_idx_ref.1, bf16[128,8,512]{2,1,0:T(8,128)(2,1)} %bitcast.10, bf16[128,4,512]{2,1,0:T(4,128)(2,1)} %reshape.105.hub_ref, bf16[128,4,512]{2,1,0:T(4,128)(2,1)} %reshape.106.term_ref, ...), custom_call_target="tpu_custom_call" | custom-call | tf_op jit(solution)/shard_map/grad_return/pallas_call | solution.py:259
  129.1 0.0 copy-start
  129.1 2.7 %reshape.108 = f32[512,512]{1,0:T(8,128)} reshape(f32[128,4,512]{2,1,0:T(4,128)} %get-tuple-element.20) | data formatting | bytes 2097152 | tf_op jit(solution)/shard_map/reshape | solution.py:299
  131.8 0.0 copy-done
  131.8 1.3 copy.21
Async XLA Ops:
  129.1 2.7 %copy-start = (bf16[2048,512]{1,0:T(8,128)(2,1)S(1)}, bf16[2048,512]{1,0:T(8,128)(2,1)}, u32[]{:S(2)}) copy-start(bf16[2048,512]{1,0:T(8,128)(2,1)} %get-tuple-element.25) | copy-start | bytes 6291460

commit v2 on v0

v2 whole, which is shorter than its diff:
```python
import jax
import jax.numpy as jnp
from jax import lax
from jax.experimental import pallas as pl
from jax.experimental.pallas import tpu as pltpu
from jax.sharding import PartitionSpec as P

MESH = pl.DeviceIdType.MESH
N = 128
CHIPS = 64
F = 512
HALF = 256
R = 2048
TILE = 128
SLOTS = 8
HUBS = 4
TILES = 96
NEAR = 64
F32 = jnp.float32
BF16 = jnp.bfloat16
LIMIT = 62 * 1024 * 1024
STEP = 4
PAIR, HUB, HALO, TERM, BACK, HUB_BACK, SHARE, PAIR_BACK = range(8)


def whole_wait(ref, sem):
    pltpu.make_async_copy(ref, ref, sem).wait()


def one_hot(index, lanes):
    return (index == lanes).astype(F32).astype(BF16)


def transposed_dot(a, b):
    return lax.dot_general(a, b, (((0,), (0,)), ((), ())), preferred_element_type=F32)


def body(
    tiles_id, links, hub_s, send_ref, count_ref, feat_hbm, weight_ref, cot_hbm, tiles_hbm,
    out_ref, gfeat_ref, gweight_ref,
    tiles, near, far, cot, sums, gagg, term, column, picks, hub_picks,
    hub_slot, hub_chip, hub_in, halo_out, halo_in,
    term_out, term_in, share, gathered, back_out, back_in,
    hub_out, hub_back, hub_pair, hub_rows,
    load, send, recv,
):
    me = lax.axis_index("dom")
    chip, core = me // 2, lax.rem(me, 2)
    sibling = me + 1 - 2 * core

    loads = (
        pltpu.make_async_copy(feat_hbm, near.at[pl.ds(0, 16)], load.at[0]),
        pltpu.make_async_copy(tiles_hbm, tiles, load.at[1]),
        pltpu.make_async_copy(cot_hbm, cot, load.at[2]),
    )
    for copy in loads:
        copy.start()

    barrier = pltpu.get_barrier_semaphore()

    @pl.loop(1, N)
    def _(i):
        pl.semaphore_signal(
            barrier, inc=1, device_id=(lax.rem(me + i, N),), device_id_type=MESH
        )

    def remote(src, dst, slot, peer):
        return pltpu.make_async_remote_copy(
            src_ref=src, dst_ref=dst, send_sem=send.at[slot], recv_sem=recv.at[slot],
            device_id=(peer,), device_id_type=MESH,
        )

    slot_iota = lax.broadcasted_iota(jnp.int32, (SLOTS, N), 0)
    index = jnp.where(slot_iota < count_ref[...], send_ref[...], -1).astype(F32)
    index = jnp.concatenate([index, jnp.zeros((N - SLOTS, N), F32)], axis=0).T
    sub = lax.broadcasted_iota(jnp.int32, (TILE, TILE), 0)
    lane = lax.broadcasted_iota(jnp.int32, (TILE, TILE), 1)
    diagonal = lane == lax.rem(sub, SLOTS)
    for b in range(8):
        spread = jnp.broadcast_to(index[16 * b : 16 * b + 16, None, :], (16, SLOTS, N))
        chosen = jnp.where(diagonal, spread.reshape(TILE, TILE), 0.0)
        one = jnp.sum(chosen, axis=1, keepdims=True)
        column[pl.ds(b * TILE, TILE), :] = jnp.broadcast_to(one, (TILE, TILE)).astype(jnp.int32)

    hub_at = lax.broadcasted_iota(jnp.int32, (8, R), 0)
    hub_id = jnp.full((8, R), -1, jnp.int32)
    for j in range(HUBS):
        hub_id = jnp.where(hub_at == HUBS * core + j, hub_s[j], hub_id)
    sums[0] = jnp.zeros((TILE, F), F32)

    loads[0].wait()
    lanes = lax.broadcasted_iota(jnp.int32, (8, R), 1)
    hub_slot[0] = jnp.dot(
        one_hot(hub_id, lanes), near[pl.ds(0, 16)].reshape(R, F), preferred_element_type=F32
    ).astype(BF16)

    lanes = lax.broadcasted_iota(jnp.int32, (HALF, R), 1)
    for b in range(4):
        here = column[pl.ds(b * HALF, HALF), 0:1]
        rows = jnp.dot(
            one_hot(here, lanes), near[pl.ds(0, 16)].reshape(R, F), preferred_element_type=F32
        )
        halo_out[pl.ds(b * 32, 32)] = rows.reshape(32, SLOTS, F).astype(BF16)

    pl.semaphore_wait(barrier, N - 1)
    pair = remote(hub_slot.at[0], hub_slot.at[1], PAIR, sibling)
    pair.start()
    pltpu.make_async_copy(halo_out.at[me], halo_in.at[me], recv.at[HALO]).start()

    @pl.loop(1, 33)
    def _(i):
        peer = lax.rem(me + i, N)
        remote(halo_out.at[peer], halo_in.at[me], HALO, peer).start()

    pair.wait()
    hub_chip[0] = hub_slot[0] + hub_slot[1]
    pltpu.make_async_copy(hub_chip.at[0], hub_in.at[chip], recv.at[HUB]).start()

    @pl.loop(1, CHIPS)
    def _(i):
        peer = lax.rem(me + 2 * i, N)
        remote(hub_chip.at[0], hub_in.at[chip], HUB, peer).start()

    @pl.loop(33, N)
    def _(i):
        peer = lax.rem(me + i, N)
        remote(halo_out.at[peer], halo_in.at[me], HALO, peer).start()

    for b in range(8):
        picks_row = column[pl.ds(b * TILE, TILE), :].astype(F32).T.astype(jnp.int32)[0:1, :]

        @pl.loop(0, 16)
        def _(k):
            here = pl.ds(pl.multiple_of(k * TILE, TILE), TILE)
            picks[here, pl.ds(b * TILE, TILE)] = one_hot(picks_row, sub + k * TILE)

    hub_lane = lax.rem(lane, 8)
    hub_row = jnp.full((TILE, TILE), -1, jnp.int32)
    for j in range(HUBS):
        hub_row = jnp.where((hub_lane == HUBS * core + j) & (lane < 16), hub_s[j], hub_row)

    @pl.loop(0, 16)
    def _(k):
        here = pl.ds(pl.multiple_of(k * TILE, TILE), TILE)
        hub_picks[here, :] = one_hot(hub_row, sub + k * TILE)

    loads[1].wait()
    whole_wait(hub_in, recv.at[HUB])
    near[pl.ds(16, 4)] = hub_in[...].reshape(4, TILE, F)

    @pl.loop(0, NEAR // STEP)
    def _(g):
        for u in range(STEP):
            t = STEP * g + u
            sums[t + 1] = sums[links[0, t]] + jnp.dot(
                tiles[t], near[tiles_id[1, t]], preferred_element_type=F32
            )

    whole_wait(halo_in, recv.at[HALO])
    far[...] = halo_in[...].reshape(8, TILE, F)

    @pl.loop(0, (TILES - NEAR) // STEP)
    def _(g):
        for u in range(STEP):
            t = NEAR + STEP * g + u
            sums[t + 1] = sums[links[0, t]] + jnp.dot(
                tiles[t], far[jnp.maximum(tiles_id[1, t] - 20, 0)], preferred_element_type=F32
            )

    loads[2].wait()
    term[...] = jnp.zeros_like(term)
    weight = weight_ref[...]

    @pl.loop(0, 4)
    def _(k):
        parts = [sums[links[0, TILES + 4 * k + j]] for j in range(4)]
        agg = jnp.concatenate(parts, axis=0).astype(BF16)
        pre = jnp.dot(agg, weight, preferred_element_type=F32)
        sig = 0.5 * jnp.tanh(0.5 * pre) + 0.5
        here = pl.ds(pl.multiple_of(k * 512, 512), 512)
        out_ref[here, :] = (pre * sig).astype(BF16)
        gpre = (cot[here, :].astype(F32) * sig * (1.0 + pre * (1.0 - sig))).astype(BF16)
        term[...] += transposed_dot(agg, gpre)
        back = lax.dot_general(gpre, weight, (((1,), (1,)), ((), ())), preferred_element_type=F32)
        gagg[pl.ds(4 * k, 4)] = back.astype(BF16).reshape(4, TILE, F)

    whole = (term[...] * (1.0 / 512.0)).reshape(CHIPS, 8, F).astype(BF16)
    term_out[0] = whole[:, :, :HALF]
    term_out[1] = whole[:, :, HALF:]
    pltpu.make_async_copy(term_out.at[core, chip], term_in.at[me], recv.at[TERM]).start()

    @pl.loop(1, N)
    def _(i):
        peer = lax.rem(me + i, N)
        remote(term_out.at[lax.rem(peer, 2), peer // 2], term_in.at[me], TERM, peer).start()

    def spread_tile(t):
        sums[t + 1] = sums[links[1, t]] + transposed_dot(tiles[t], gagg[tiles_id[0, t]])

    @pl.loop(0, (TILES - NEAR) // STEP)
    def _(g):
        for u in range(STEP):
            spread_tile(NEAR + STEP * g + u)

    for b in range(8):
        rows = sums[links[1, TILES + 20 + b]]
        back_out[pl.ds(16 * b, 16)] = rows.reshape(16, SLOTS, F).astype(BF16)
    pltpu.make_async_copy(back_out.at[me], back_in.at[me], recv.at[BACK]).start()

    @pl.loop(1, N)
    def _(i):
        peer = lax.rem(me + i, N)
        remote(back_out.at[peer], back_in.at[me], BACK, peer).start()

    @pl.loop(0, NEAR // STEP)
    def _(g):
        for u in range(STEP):
            spread_tile(STEP * g + u)

    for b in range(4):
        rows = sums[links[1, TILES + 16 + b]].reshape(16, 8, F).astype(BF16)
        hub_out[0, pl.ds(16 * b, 16)] = rows[:, :, :HALF]
        hub_out[1, pl.ds(16 * b, 16)] = rows[:, :, HALF:]
    pltpu.make_async_copy(hub_out.at[core, chip], hub_back.at[me], recv.at[HUB_BACK]).start()

    @pl.loop(1, N)
    def _(i):
        peer = lax.rem(me + i, N)
        remote(hub_out.at[lax.rem(peer, 2), peer // 2], hub_back.at[me], HUB_BACK, peer).start()

    whole_wait(term_in, recv.at[TERM])
    share[0] = jnp.sum(term_in[...].astype(F32), axis=0).astype(BF16)
    pltpu.make_async_copy(share.at[0], gathered.at[core, chip], recv.at[SHARE]).start()

    @pl.loop(1, N)
    def _(i):
        peer = lax.rem(me + i, N)
        remote(share.at[0], gathered.at[core, chip], SHARE, peer).start()

    whole_wait(back_in, recv.at[BACK])

    @pl.loop(0, 8)
    def _(k):
        here = pl.ds(pl.multiple_of(k * HALF, HALF), HALF)
        back = jnp.dot(
            picks[here, :], back_in[...].reshape(N * SLOTS, F), preferred_element_type=F32
        )
        for j in range(2):
            at = links[1, TILES + 2 * k + j]
            sums[2 * k + j + 1 + 100] = sums[at] + back[j * TILE : j * TILE + TILE]

    whole_wait(hub_back, recv.at[HUB_BACK])
    hub_pair[0] = jnp.sum(hub_back[...].astype(F32), axis=0)
    pair = remote(hub_pair.at[0], hub_pair.at[1], PAIR_BACK, sibling)
    pair.start()
    pair.wait()
    hub_rows[...] = jnp.zeros_like(hub_rows)
    first = jnp.where(core == 0, hub_pair[0], hub_pair[1])
    second = jnp.where(core == 0, hub_pair[1], hub_pair[0])
    total = jnp.concatenate([first, second], axis=1)
    upper = total.astype(BF16).astype(F32)
    hub_rows[pl.ds(0, 16), :] = jnp.concatenate([upper, total - upper], axis=0).astype(BF16)

    @pl.loop(0, 8)
    def _(k):
        here = pl.ds(pl.multiple_of(k * HALF, HALF), HALF)
        hub = jnp.dot(hub_picks[here, :], hub_rows[...], preferred_element_type=F32)
        mine = sums[pl.ds(2 * k + 101, 2)].reshape(HALF, F)
        gfeat_ref[here, :] = (mine + hub).astype(BF16)

    whole_wait(gathered, recv.at[SHARE])
    for q in range(2):
        gweight_ref[:, :, q * HALF : q * HALF + HALF] = gathered[q].astype(F32)

    whole_wait(hub_in.at[pl.ds(0, CHIPS - 1)], send.at[HUB])
    whole_wait(halo_in.at[pl.ds(0, N - 1)], send.at[HALO])
    whole_wait(term_in.at[pl.ds(0, N - 1)], send.at[TERM])
    whole_wait(back_in.at[pl.ds(0, N - 1)], send.at[BACK])
    whole_wait(hub_back.at[pl.ds(0, N - 1)], send.at[HUB_BACK])
    whole_wait(term_in.at[pl.ds(0, N - 1)], send.at[SHARE])


def per_device(
    features, weight, cotangent, tile_values, tile_rows, tile_cols, hub_rows, send_rows, send_count
):
    ids = jnp.stack([tile_rows, tile_cols])
    blocks = jnp.broadcast_to(jnp.arange(32, dtype=jnp.int32), (2, 32))
    asked = jnp.concatenate([ids, blocks], axis=1)
    place = jnp.minimum(jnp.arange(128, dtype=jnp.int32), TILES)
    number = jnp.arange(TILES, dtype=jnp.int32)
    before = (ids[:, None, :] == asked[:, :, None]) & (number[None, :] < place[:, None])
    links = jnp.max(jnp.where(before, number + 1, 0), axis=2)

    smem = pl.BlockSpec(memory_space=pltpu.SMEM)
    vmem = pl.BlockSpec(memory_space=pltpu.VMEM)
    anywhere = pl.BlockSpec(memory_space=pl.ANY)
    output, grad_features, grad_weight = pl.pallas_call(
        body,
        out_shape=(
            jax.ShapeDtypeStruct((R, F), BF16),
            jax.ShapeDtypeStruct((R, F), BF16),
            jax.ShapeDtypeStruct((CHIPS, 8, F), F32),
        ),
        in_specs=[smem] * 3 + [vmem] * 2 + [anywhere, vmem, anywhere, anywhere],
        out_specs=(vmem, vmem, vmem),
        scratch_shapes=[
            pltpu.VMEM((TILES, TILE, TILE), BF16),
            pltpu.VMEM((20, TILE, F), BF16),
            pltpu.VMEM((8, TILE, F), BF16),
            pltpu.VMEM((R, F), BF16),
            pltpu.VMEM((TILES + 21, TILE, F), F32),
            pltpu.VMEM((16, TILE, F), BF16),
            pltpu.VMEM((F, F), F32),
            pltpu.VMEM((N * SLOTS, TILE), jnp.int32),
            pltpu.VMEM((R, N * SLOTS), BF16),
            pltpu.VMEM((R, TILE), BF16),
            pltpu.VMEM((2, 8, F), BF16),
            pltpu.VMEM((1, 8, F), BF16),
            pltpu.VMEM((CHIPS, 8, F), BF16),
            pltpu.VMEM((N, SLOTS, F), BF16),
            pltpu.VMEM((N, SLOTS, F), BF16),
            pltpu.VMEM((2, CHIPS, 8, HALF), BF16),
            pltpu.VMEM((N, 8, HALF), BF16),
            pltpu.VMEM((1, 8, HALF), BF16),
            pltpu.VMEM((2, CHIPS, 8, HALF), BF16),
            pltpu.VMEM((N, SLOTS, F), BF16),
            pltpu.VMEM((N, SLOTS, F), BF16),
            pltpu.VMEM((2, CHIPS, 8, HALF), BF16),
            pltpu.VMEM((N, 8, HALF), BF16),
            pltpu.VMEM((2, 8, HALF), F32),
            pltpu.VMEM((TILE, F), BF16),
            pltpu.SemaphoreType.DMA((3,)),
            pltpu.SemaphoreType.DMA((8,)),
            pltpu.SemaphoreType.DMA((8,)),
        ],
        compiler_params=pltpu.CompilerParams(
            collective_id=0, has_side_effects=True, vmem_limit_bytes=LIMIT
        ),
        name="graph_layer",
    )(
        ids, links, hub_rows, send_rows[0].T, send_count, features.reshape(16, TILE, F), weight,
        cotangent, tile_values,
    )
    return output, grad_features, grad_weight.reshape(F, F)


def solution(mesh):
    placed = (
        P("dom", None),
        P(),
        P("dom", None),
        P("dom", None, None),
        P("dom"),
        P("dom"),
        P("dom"),
        P("dom", None, None),
        P("dom", None),
    )
    return jax.shard_map(
        per_device,
        mesh=mesh,
        in_specs=placed,
        out_specs=(P("dom", None), P("dom", None), P()),
        check_vma=False,
    )
```

time: 438 us -> 90.4 us (0.21)
  matrix products: 154 us -> 0 us
  waiting for transfers between devices: 141 us -> 0 us
  Pallas kernels: 0 us -> 81.3 us
  local copies, waits for them, and re-layouts: 61.2 us -> 6.13 us
  blocking collectives: 45.4 us -> 0 us
  starting transfers between devices: 16.9 us -> 0 us
  between operations: 14.8 us -> 0.68 us
    dot_general x33 -> x0, matrix products: 154 us -> none  [the longest x8 55.5 us: add_into(): jnp.einsum('kr,kif->rif', selector, upper, preferred_element_type=jnp.flo...]
    unnamed x2 -> x0, waiting for transfers between devices: 141 us -> none
    pallas_call x0 -> x1, Pallas kernels: none -> 81.3 us  [per_device(): pl.pallas_call(body, out_shape=(jax.ShapeDtypeStruct((R, F), BF16), jax.S...]
    all_gather x1 -> x0, blocking collectives: 45.4 us -> none  [per_device(): hub_all = lax.all_gather(hub_local, 'dom', axis=0, tiled=True)]
    convert_element_type x7 -> x0, local copies, waits for them, and re-layouts: 34.3 us -> none  [the longest x2 15.9 us: add_into(): upper = terms.astype(jnp.bfloat16)]
    all_to_all x2 -> x0, starting transfers between devices: 16.9 us -> none  [the longest x1 12 us: per_device(): lax.all_to_all(outgoing, 'dom', split_axis=0, concat_axis=0, tiled=True)]
    slice x7 -> x0, local copies, waits for them, and re-layouts: 9.22 us -> none  [the longest x2 4.85 us: per_device(): own_grad = near_flat[:row_count]]
    while x5 -> x0, local copies, waits for them, and re-layouts: 6.55 us -> none  [the longest x1 5.97 us: spread_tiles(): result, _ = lax.scan(spread_advance, running, packed)]
  transfers between devices with their start and end apart: 3 -> 0, of which waited for: 1 -> 0; matrix products, arithmetic and copies ran while one was open for 28% -> 0% of each run, Pallas kernels for 0% -> 0%
where the time goes in v2:
time: 90.4 us; the launch traced here: 90.2 us
  Pallas kernels  81.3 us (90%)
  local copies, waits for them, and re-layouts  6.13 us (7%)
  other arithmetic  2.13 us (2%)
    pallas_call x1, Pallas kernels, per_device(): pl.pallas_call(body, out_shape=(jax.ShapeDtypeStruct((R, F), BF16), jax.S...  81.3 us
    unnamed x9, local copies, waits for them, and re-layouts  6.13 us

profile of v2, /device:TPU:1, one launch (start us, length us, event | category | flops | bytes accessed | tf_op | source)
XLA Modules:
  0.0 90.2 jit_solution(1174575481285056800)
XLA Ops:
  0.7 0.7 pad_add_fusion.tiles_id
  1.3 0.0 copy-start.2
  1.3 0.7 pad_add_fusion.1
  2.1 0.7 select_reduce_fusion.links
  2.8 0.0 copy-done.2
  2.8 81.3 %graph_layer.1 = (bf16[2048,512]{1,0:T(8,128)(2,1)}, bf16[2048,512]{1,0:T(8,128)(2,1)}, f32[64,8,512]{2,1,0:T(8,128)}) custom-call(s32[2,96]{1,0:T(2,128)} %copy-done.2, s32[2,128]{1,0:T(2,128)} %select_reduce_fusion.links, s32[4]{0:T(128)} %hub_s.1, s32[8,128]{1,0:T(8,128)} %bitcast.9, s32[1,128]{1,0:T(1,128)} %count_ref.1, bf16[16,128,512]{2,1,0:T(8,128)(2,1)} %bitcast.7, ...), custom_call_target="tpu_custom_call" | custom-call | tf_op jit(solution)/shard_map/graph_layer/pallas_call | solution.py:297
  84.1 0.0 copy-start
  84.1 3.2 %copy.15 = bf16[2048,512]{1,0:T(8,128)(2,1)} copy(bf16[2048,512]{1,0:T(8,128)(2,1)} %get-tuple-element.12) | data formatting | bytes 4194304
  87.3 0.0 copy-done
  87.3 0.0 copy-start.1
  87.3 1.3 %copy.16 = bf16[2048,512]{1,0:T(8,128)(2,1)} copy(bf16[2048,512]{1,0:T(8,128)(2,1)S(1)} %copy-done) | data formatting | bytes 4194304
  88.6 0.6 copy-done.1
  89.2 1.0 %copy.17 = f32[512,512]{1,0:T(8,128)} copy(f32[512,512]{1,0:T(8,128)S(1)} %bitcast.8) | data formatting | bytes 2097152
  (4 shorter events, 0.0 us)
Async XLA Ops:
  1.3 1.5 %copy-start.2 = (s32[2,96]{1,0:T(2,128)}, s32[2,96]{1,0:T(2,128)S(1)}, u32[]{:S(2)}) copy-start(s32[2,96]{1,0:T(2,128)S(1)} %pad_add_fusion.tiles_id) | copy-start | bytes 2308
  84.1 3.2 %copy-start = (bf16[2048,512]{1,0:T(8,128)(2,1)S(1)}, bf16[2048,512]{1,0:T(8,128)(2,1)}, u32[]{:S(2)}) copy-start(bf16[2048,512]{1,0:T(8,128)(2,1)} %get-tuple-element.13) | copy-start | bytes 6291460
  87.3 2.0 %copy-start.1 = (f32[64,8,512]{2,1,0:T(8,128)S(1)}, f32[64,8,512]{2,1,0:T(8,128)}, u32[]{:S(2)}) copy-start(f32[64,8,512]{2,1,0:T(8,128)} %get-tuple-element.8) | copy-start | bytes 3145732

commit v3 on v2

v3 whole, which is shorter than its diff:
```python
import jax
import jax.numpy as jnp
from jax import lax
from jax.experimental import pallas as pl
from jax.experimental.pallas import tpu as pltpu
from jax.sharding import PartitionSpec as P

MESH = pl.DeviceIdType.MESH
N = 128
CHIPS = 64
F = 512
HALF = 256
R = 2048
TILE = 128
SLOTS = 8
HUBS = 4
TILES = 96
NEAR = 64
F32 = jnp.float32
BF16 = jnp.bfloat16
LIMIT = 62 * 1024 * 1024
STEP = 4
(
    PAIR, HUB, HUB_SHARE, HALO, TERM_PAIR, TERM, BACK, BACK_PAIR, HUB_BACK, SHARE, SHARE_PAIR,
    LAST_PAIR,
) = range(12)
MORE = TILES + 1


def whole_wait(ref, sem):
    pltpu.make_async_copy(ref, ref, sem).wait()


def one_hot(index, lanes):
    return (index == lanes).astype(F32).astype(BF16)


def transposed_dot(a, b):
    return lax.dot_general(a, b, (((0,), (0,)), ((), ())), preferred_element_type=F32)


def body(
    rows_s, cols_s, hub_s, rows_ref, cols_ref, send_ref, count_ref, feat_hbm, weight_ref, cot_hbm,
    tiles_hbm,
    out_hbm, gfeat_hbm, gweight_hbm,
    tiles, near, far, cot, out, sums, gagg, term, turned, column, picks, hub_picks, ids, links_v,
    hub_own, hub_got, hub_half, hub_in, halo_out, halo_in,
    term_out, term_got, term_half, term_in, share, gathered, back_out, back_in,
    hub_out, hub_back_got, hub_back_half, hub_back, hub_pair, hub_rows,
    links, load, store, send, recv,
):
    me = lax.axis_index("dom")
    chip, core = me // 2, lax.rem(me, 2)
    sibling = me + 1 - 2 * core
    other = 1 - core

    loads = (
        pltpu.make_async_copy(feat_hbm, near.at[pl.ds(0, 16)], load.at[0]),
        pltpu.make_async_copy(tiles_hbm, tiles, load.at[1]),
        pltpu.make_async_copy(cot_hbm, cot, load.at[2]),
    )
    for copy in loads:
        copy.start()

    barrier = pltpu.get_barrier_semaphore()

    @pl.loop(1, N)
    def _(i):
        pl.semaphore_signal(
            barrier, inc=1, device_id=(lax.rem(me + i, N),), device_id_type=MESH
        )

    def remote(src, dst, slot, peer):
        return pltpu.make_async_remote_copy(
            src_ref=src, dst_ref=dst, send_sem=send.at[slot], recv_sem=recv.at[slot],
            device_id=(peer,), device_id_type=MESH,
        )

    def link(q, t):
        return jnp.clip(links[q, t], 0, TILES)

    def to_plane(source, target, slot):
        @pl.loop(1, CHIPS)
        def _(j):
            there = lax.rem(chip + 23 * j, CHIPS)
            remote(source(there), target, slot, 2 * there + core).start()

    slot_iota = lax.broadcasted_iota(jnp.int32, (SLOTS, N), 0)
    index = jnp.where(slot_iota < count_ref[...], send_ref[...], -1).astype(F32)
    turned[...] = jnp.concatenate([index, jnp.zeros((N - SLOTS, N), F32)], axis=0).T
    sub = lax.broadcasted_iota(jnp.int32, (TILE, TILE), 0)
    lane = lax.broadcasted_iota(jnp.int32, (TILE, TILE), 1)
    diagonal = lax.broadcasted_iota(jnp.int32, (HALF, TILE), 1) == lax.rem(
        lax.broadcasted_iota(jnp.int32, (HALF, TILE), 0), SLOTS
    )
    for b in range(4):
        part = turned[pl.ds(b, 32, stride=4), :]
        spread = jnp.broadcast_to(part[:, None, :], (32, SLOTS, N)).reshape(HALF, TILE)
        one = jnp.sum(jnp.where(diagonal, spread, 0.0), axis=1, keepdims=True)
        column[pl.ds(b * HALF, HALF), :] = jnp.broadcast_to(one, (HALF, TILE)).astype(jnp.int32)

    hub_at = lax.broadcasted_iota(jnp.int32, (8, R), 0)
    hub_id = jnp.full((8, R), -1, jnp.int32)
    for j in range(HUBS):
        hub_id = jnp.where(hub_at == HUBS * core + j, hub_s[j], hub_id)

    loads[0].wait()
    lanes = lax.broadcasted_iota(jnp.int32, (8, R), 1)
    rows = jnp.dot(
        one_hot(hub_id, lanes), near[pl.ds(0, 16)].reshape(R, F), preferred_element_type=F32
    ).astype(BF16)
    hub_own[0] = rows[:, :HALF]
    hub_own[1] = rows[:, HALF:]

    def gather(block):
        here = column[pl.ds(pl.multiple_of(block * HALF, HALF), HALF), 0:1]
        rows = jnp.dot(
            one_hot(here, lax.broadcasted_iota(jnp.int32, (HALF, R), 1)),
            near[pl.ds(0, 16)].reshape(R, F), preferred_element_type=F32,
        )
        halo_out[block] = rows.reshape(32, SLOTS, F).astype(BF16)

    def send_block(block, first):
        @pl.loop(first, 32)
        def _(j):
            there = lax.rem(me // 4 + 11 * j, 32)
            remote(
                halo_out.at[block, there], halo_in.at[me], HALO, 4 * there + block
            ).start()

    quarter = lax.rem(me, 4)
    gather(quarter)
    pl.semaphore_wait(barrier, N - 1)
    pair = remote(hub_own.at[other], hub_got.at[0], PAIR, sibling)
    pair.start()
    pltpu.make_async_copy(halo_out.at[quarter, me // 4], halo_in.at[me], recv.at[HALO]).start()
    send_block(quarter, 1)
    gather(lax.rem(quarter + 1, 4))
    pair.wait()
    hub_half[0] = hub_own[core] + hub_got[0]
    pltpu.make_async_copy(hub_half.at[0], hub_in.at[core, chip], recv.at[HUB]).start()
    to_plane(lambda there: hub_half.at[0], hub_in.at[core, chip], HUB)
    send_block(lax.rem(quarter + 1, 4), 0)
    for b in range(2, 4):
        gather(lax.rem(quarter + b, 4))
        send_block(lax.rem(quarter + b, 4), 0)

    ids[...] = jnp.zeros_like(ids)
    ids[0:1, 0:TILES] = rows_ref[...]
    ids[1:2, 0:TILES] = cols_ref[...]
    links_v[...] = jnp.zeros_like(links_v)
    for q in range(2):
        keys = jnp.broadcast_to(ids[q : q + 1, :], (TILE, TILE))
        asked = jnp.where(lane < TILES, keys, lane - TILES)
        before = (keys.T == asked) & (sub < jnp.minimum(lane, TILES))
        number = jnp.where(before, sub + 1, 0)
        links_v[q : q + 1, :] = jnp.max(number, axis=0, keepdims=True)
    copy_links = pltpu.make_async_copy(links_v, links, load.at[3])
    copy_links.start()
    sums[0] = jnp.zeros((TILE, F), F32)

    for b in range(8):
        picks_row = column[pl.ds(b * TILE, TILE), :].astype(F32).T.astype(jnp.int32)[0:1, :]

        @pl.loop(0, 16)
        def _(k):
            here = pl.ds(pl.multiple_of(k * TILE, TILE), TILE)
            picks[here, pl.ds(b * TILE, TILE)] = one_hot(picks_row, sub + k * TILE)

    hub_lane = lax.rem(lane, 8)
    hub_row = jnp.full((TILE, TILE), -1, jnp.int32)
    for j in range(HUBS):
        hub_row = jnp.where((hub_lane == HUBS * core + j) & (lane < 16), hub_s[j], hub_row)

    @pl.loop(0, 16)
    def _(k):
        here = pl.ds(pl.multiple_of(k * TILE, TILE), TILE)
        hub_picks[here, :] = one_hot(hub_row, sub + k * TILE)

    whole_wait(hub_in.at[core], recv.at[HUB])
    pair = remote(hub_in.at[core], hub_in.at[core], HUB_SHARE, sibling)
    pair.start()
    loads[1].wait()
    copy_links.wait()
    pair.wait()
    for b in range(4):
        for q in range(2):
            near[16 + b, :, q * HALF : q * HALF + HALF] = hub_in[q, pl.ds(16 * b, 16)].reshape(
                TILE, HALF
            )

    @pl.loop(0, NEAR // STEP)
    def _(g):
        for u in range(STEP):
            t = STEP * g + u
            sums[t + 1] = sums[link(0, t)] + jnp.dot(
                tiles[t], near[cols_s[t]], preferred_element_type=F32
            )

    whole_wait(halo_in, recv.at[HALO])
    far[...] = halo_in[...].reshape(8, TILE, F)

    @pl.loop(0, (TILES - NEAR) // STEP)
    def _(g):
        for u in range(STEP):
            t = NEAR + STEP * g + u
            sums[t + 1] = sums[link(0, t)] + jnp.dot(
                tiles[t], far[jnp.maximum(cols_s[t] - 20, 0)], preferred_element_type=F32
            )

    loads[2].wait()
    term[...] = jnp.zeros_like(term)
    weight = weight_ref[...]

    @pl.loop(0, 4)
    def _(k):
        parts = [sums[link(0, TILES + 4 * k + j)] for j in range(4)]
        agg = jnp.concatenate(parts, axis=0).astype(BF16)
        pre = jnp.dot(agg, weight, preferred_element_type=F32)
        sig = 0.5 * jnp.tanh(0.5 * pre) + 0.5
        here = pl.ds(pl.multiple_of(k * 512, 512), 512)
        out[here, :] = (pre * sig).astype(BF16)
        gpre = (cot[here, :].astype(F32) * sig * (1.0 + pre * (1.0 - sig))).astype(BF16)
        term[...] += transposed_dot(agg, gpre)
        back = lax.dot_general(gpre, weight, (((1,), (1,)), ((), ())), preferred_element_type=F32)
        gagg[pl.ds(4 * k, 4)] = back.astype(BF16).reshape(4, TILE, F)

    save_out = pltpu.make_async_copy(out, out_hbm, store.at[0])
    save_out.start()
    whole = (term[...] * (1.0 / 512.0)).reshape(CHIPS, 8, F).astype(BF16)
    term_out[0] = whole[:, :, :HALF]
    term_out[1] = whole[:, :, HALF:]
    pair = remote(term_out.at[other], term_got, TERM_PAIR, sibling)
    pair.start()

    def spread_tile(t):
        sums[t + 1] = sums[link(1, t)] + transposed_dot(tiles[t], gagg[rows_s[t]])

    @pl.loop(0, 16 // STEP)
    def _(g):
        for u in range(STEP):
            spread_tile(NEAR + STEP * g + u)

    pair.wait()
    term_half[...] = (term_out[core].astype(F32) + term_got[...].astype(F32)).astype(BF16)
    pltpu.make_async_copy(term_half.at[chip], term_in.at[chip], recv.at[TERM]).start()
    to_plane(lambda there: term_half.at[there], term_in.at[chip], TERM)

    @pl.loop(16 // STEP, (TILES - NEAR) // STEP)
    def _(g):
        for u in range(STEP):
            spread_tile(NEAR + STEP * g + u)

    for b in range(8):
        rows = sums[link(1, TILES + 20 + b)]
        back_out[pl.ds(16 * b, 16)] = rows.reshape(16, SLOTS, F).astype(BF16)
    landing = back_in.at[quarter, me // 4]
    pltpu.make_async_copy(back_out.at[me], landing, recv.at[BACK]).start()

    @pl.loop(1, N)
    def _(i):
        peer = lax.rem(me + 37 * i, N)
        remote(back_out.at[peer], landing, BACK, peer).start()

    @pl.loop(0, NEAR // STEP)
    def _(g):
        for u in range(STEP):
            spread_tile(STEP * g + u)

    for b in range(4):
        rows = sums[link(1, TILES + 16 + b)].reshape(16, 8, F).astype(BF16)
        hub_out[0, pl.ds(16 * b, 16)] = rows[:, :, :HALF]
        hub_out[1, pl.ds(16 * b, 16)] = rows[:, :, HALF:]
    pair = remote(hub_out.at[other], hub_back_got, BACK_PAIR, sibling)
    pair.start()

    whole_wait(term_in, recv.at[TERM])
    share[0] = jnp.sum(term_in[...].astype(F32), axis=0).astype(BF16)
    pltpu.make_async_copy(share.at[0], gathered.at[core, chip], recv.at[SHARE]).start()
    to_plane(lambda there: share.at[0], gathered.at[core, chip], SHARE)

    pair.wait()
    hub_back_half[...] = (
        hub_out[core].astype(F32) + hub_back_got[...].astype(F32)
    ).astype(BF16)
    pltpu.make_async_copy(hub_back_half.at[chip], hub_back.at[chip], recv.at[HUB_BACK]).start()
    to_plane(lambda there: hub_back_half.at[there], hub_back.at[chip], HUB_BACK)

    whole_wait(back_in, recv.at[BACK])

    @pl.loop(0, 8)
    def _(k):
        here = pl.ds(pl.multiple_of(k * HALF, HALF), HALF)
        back = jnp.dot(
            picks[here, :], back_in[...].reshape(N * SLOTS, F), preferred_element_type=F32
        )
        for j in range(2):
            at = link(1, TILES + 2 * k + j)
            sums[2 * k + j + MORE] = sums[at] + back[j * TILE : j * TILE + TILE]

    whole_wait(gathered.at[core], recv.at[SHARE])
    share_pair = remote(gathered.at[core], gathered.at[core], SHARE_PAIR, sibling)
    share_pair.start()

    whole_wait(hub_back, recv.at[HUB_BACK])
    hub_pair[0] = jnp.sum(hub_back[...].astype(F32), axis=0)
    pair = remote(hub_pair.at[0], hub_pair.at[1], LAST_PAIR, sibling)
    pair.start()
    save_out.wait()
    share_pair.wait()
    save_weight = pltpu.make_async_copy(gathered, gweight_hbm, store.at[1])
    save_weight.start()
    pair.wait()
    hub_rows[...] = jnp.zeros_like(hub_rows)
    first = jnp.where(core == 0, hub_pair[0], hub_pair[1])
    second = jnp.where(core == 0, hub_pair[1], hub_pair[0])
    total = jnp.concatenate([first, second], axis=1)
    upper = total.astype(BF16).astype(F32)
    hub_rows[pl.ds(0, 16), :] = jnp.concatenate([upper, total - upper], axis=0).astype(BF16)

    @pl.loop(0, 8)
    def _(k):
        here = pl.ds(pl.multiple_of(k * HALF, HALF), HALF)
        hub = jnp.dot(hub_picks[here, :], hub_rows[...], preferred_element_type=F32)
        mine = sums[pl.ds(2 * k + MORE, 2)].reshape(HALF, F)
        out[here, :] = (mine + hub).astype(BF16)

    save_grad = pltpu.make_async_copy(out, gfeat_hbm, store.at[0])
    save_grad.start()
    whole_wait(hub_back.at[pl.ds(0, CHIPS - 1)], send.at[HUB])
    whole_wait(halo_in.at[pl.ds(0, N - 1)], send.at[HALO])
    whole_wait(hub_back.at[pl.ds(0, CHIPS - 1)], send.at[TERM])
    whole_wait(halo_in.at[pl.ds(0, N - 1)], send.at[BACK])
    whole_wait(hub_back.at[pl.ds(0, CHIPS - 1)], send.at[HUB_BACK])
    whole_wait(hub_back.at[pl.ds(0, CHIPS - 1)], send.at[SHARE])
    save_grad.wait()
    save_weight.wait()


def finish(out_in, gfeat_in, gathered_ref, out_ref, gfeat_ref, gweight_ref, sems):
    copies = []
    for a, (src, dst) in enumerate(((out_in, out_ref), (gfeat_in, gfeat_ref))):
        for b in range(4):
            here = pl.ds(b * 512, 512)
            copies.append(pltpu.make_async_copy(src.at[here], dst.at[here], sems.at[4 * a + b]))
    for copy in copies:
        copy.start()
    for q in range(2):
        gweight_ref[:, :, q * HALF : q * HALF + HALF] = gathered_ref[q].astype(F32)
    for copy in copies:
        copy.wait()


def per_device(
    features, weight, cotangent, tile_values, tile_rows, tile_cols, hub_rows, send_rows, send_count
):
    smem = pl.BlockSpec(memory_space=pltpu.SMEM)
    vmem = pl.BlockSpec(memory_space=pltpu.VMEM)
    anywhere = pl.BlockSpec(memory_space=pl.ANY)
    plane = (2, CHIPS, 8, HALF)
    output, grad_features, gathered = pl.pallas_call(
        body,
        out_shape=(
            jax.ShapeDtypeStruct((R, F), BF16),
            jax.ShapeDtypeStruct((R, F), BF16),
            jax.ShapeDtypeStruct(plane, BF16),
        ),
        in_specs=[smem] * 3 + [vmem] * 4 + [anywhere, vmem, anywhere, anywhere],
        out_specs=(anywhere,) * 3,
        scratch_shapes=[
            pltpu.VMEM((TILES, TILE, TILE), BF16),
            pltpu.VMEM((20, TILE, F), BF16),
            pltpu.VMEM((8, TILE, F), BF16),
            pltpu.VMEM((R, F), BF16),
            pltpu.VMEM((R, F), BF16),
            pltpu.VMEM((MORE + 16, TILE, F), F32),
            pltpu.VMEM((16, TILE, F), BF16),
            pltpu.VMEM((F, F), F32),
            pltpu.VMEM((TILE, TILE), F32),
            pltpu.VMEM((N * SLOTS, TILE), jnp.int32),
            pltpu.VMEM((R, N * SLOTS), BF16),
            pltpu.VMEM((R, TILE), BF16),
            pltpu.VMEM((8, TILE), jnp.int32),
            pltpu.VMEM((8, TILE), jnp.int32),
            pltpu.VMEM((2, 8, HALF), BF16),
            pltpu.VMEM((1, 8, HALF), BF16),
            pltpu.VMEM((1, 8, HALF), BF16),
            pltpu.VMEM(plane, BF16),
            pltpu.VMEM((4, 32, SLOTS, F), BF16),
            pltpu.VMEM((N, SLOTS, F), BF16),
            pltpu.VMEM(plane, BF16),
            pltpu.VMEM(plane[1:], BF16),
            pltpu.VMEM(plane[1:], BF16),
            pltpu.VMEM(plane[1:], BF16),
            pltpu.VMEM((1, 8, HALF), BF16),
            pltpu.VMEM(plane, BF16),
            pltpu.VMEM((N, SLOTS, F), BF16),
            pltpu.VMEM((4, 32, SLOTS, F), BF16),
            pltpu.VMEM(plane, BF16),
            pltpu.VMEM(plane[1:], BF16),
            pltpu.VMEM(plane[1:], BF16),
            pltpu.VMEM(plane[1:], BF16),
            pltpu.VMEM((2, 8, HALF), F32),
            pltpu.VMEM((TILE, F), BF16),
            pltpu.SMEM((8, TILE), jnp.int32),
            pltpu.SemaphoreType.DMA((4,)),
            pltpu.SemaphoreType.DMA((2,)),
            pltpu.SemaphoreType.DMA((12,)),
            pltpu.SemaphoreType.DMA((12,)),
        ],
        compiler_params=pltpu.CompilerParams(
            collective_id=0, has_side_effects=True, vmem_limit_bytes=LIMIT
        ),
        name="graph_layer",
    )(
        tile_rows, tile_cols, hub_rows, tile_rows.reshape(1, TILES), tile_cols.reshape(1, TILES),
        send_rows[0].T, send_count, features.reshape(16, TILE, F), weight, cotangent, tile_values,
    )
    output, grad_features, grad_weight = pl.pallas_call(
        finish,
        out_shape=(
            jax.ShapeDtypeStruct((R, F), BF16),
            jax.ShapeDtypeStruct((R, F), BF16),
            jax.ShapeDtypeStruct((CHIPS, 8, F), F32),
        ),
        in_specs=[anywhere, anywhere, vmem],
        out_specs=(anywhere, anywhere, vmem),
        scratch_shapes=[pltpu.SemaphoreType.DMA((8,))],
        name="finish",
    )(output, grad_features, gathered)
    return output, grad_features, grad_weight.reshape(F, F)


def solution(mesh):
    placed = (
        P("dom", None),
        P(),
        P("dom", None),
        P("dom", None, None),
        P("dom"),
        P("dom"),
        P("dom"),
        P("dom", None, None),
        P("dom", None),
    )
    return jax.shard_map(
        per_device,
        mesh=mesh,
        in_specs=placed,
        out_specs=(P("dom", None), P("dom", None), P()),
        check_vma=False,
    )
```

time: 90.4 us -> 200 us (2.21)
  Pallas kernels: 81.3 us -> 199 us
  local copies, waits for them, and re-layouts: 6.13 us -> 0 us
  other arithmetic: 2.13 us -> 0 us
    pallas_call x0 -> x1, Pallas kernels: none -> 130 us  [per_device(): pl.pallas_call(finish, out_shape=(jax.ShapeDtypeStruct((R, F), BF16), jax...]
    pallas_call x1, Pallas kernels: 81.3 us -> 69.2 us  [per_device(): pl.pallas_call(body, out_shape=(jax.ShapeDtypeStruct((R, F), BF16), jax.S...]
    unnamed x9 -> x0, local copies, waits for them, and re-layouts: 6.13 us -> none
where the time goes in v3:
time: 200 us
  Pallas kernels  199 us (100%)
    pallas_call x1, Pallas kernels, per_device(): pl.pallas_call(finish, out_shape=(jax.ShapeDtypeStruct((R, F), BF16), jax...  130 us
    pallas_call x1, Pallas kernels, per_device(): pl.pallas_call(body, out_shape=(jax.ShapeDtypeStruct((R, F), BF16), jax.S...  69.2 us

profile of v3, /device:TPU:1, one launch (start us, length us, event | category | flops | bytes accessed | tf_op | source)
XLA Modules:
  0.0 200.1 jit_solution(2686947363143598109)
XLA Ops:
  0.6 69.2 %graph_layer.1 = (bf16[2048,512]{1,0:T(8,128)(2,1)}, bf16[2048,512]{1,0:T(8,128)(2,1)}, bf16[2,64,8,256]{3,2,1,0:T(8,128)(2,1)}) custom-call(s32[96]{0:T(128)} %rows_s.1, s32[96]{0:T(128)} %cols_s.1, s32[4]{0:T(128)} %hub_s.1, s32[1,96]{1,0:T(1,128)} %bitcast.9, s32[1,96]{1,0:T(1,128)} %bitcast.10, s32[8,128]{1,0:T(8,128)} %bitcast.8, s32[1,128]{1,0:T(1,128)} %count_ref.1, ...), custom_call_target="tpu_custom_call" | custom-call | tf_op jit(solution)/shard_map/graph_layer/pallas_call | solution.py:361
  69.9 130.2 %finish.1 = (bf16[2048,512]{1,0:T(8,128)(2,1)}, bf16[2048,512]{1,0:T(8,128)(2,1)}, f32[64,8,512]{2,1,0:T(8,128)}) custom-call(bf16[2048,512]{1,0:T(8,128)(2,1)} %get-tuple-element.9.out_in, bf16[2048,512]{1,0:T(8,128)(2,1)} %get-tuple-element.10.gfeat_in, bf16[2,64,8,256]{3,2,1,0:T(8,128)(2,1)} %get-tuple-element.11.gathered_ref), custom_call_target="tpu_custom_call" | custom-call | tf_op jit(solution)/shard_map/finish/pallas_call | solution.py:419

commit v4 on v3

--- a/solution.py
+++ b/solution.py
@@ -19,7 +19,7 @@
 F32 = jnp.float32
 BF16 = jnp.bfloat16
 LIMIT = 62 * 1024 * 1024
-STEP = 4
+STEP = 8
 (
     PAIR, HUB, HUB_SHARE, HALO, TERM_PAIR, TERM, BACK, BACK_PAIR, HUB_BACK, SHARE, SHARE_PAIR,
     LAST_PAIR,
@@ -46,7 +46,7 @@
     tiles, near, far, cot, out, sums, gagg, term, turned, column, picks, hub_picks, ids, links_v,
     hub_own, hub_got, hub_half, hub_in, halo_out, halo_in,
     term_out, term_got, term_half, term_in, share, gathered, back_out, back_in,
-    hub_out, hub_back_got, hub_back_half, hub_back, hub_pair, hub_rows,
+    hub_back_got, hub_back_half, hub_back, hub_pair, hub_rows,
     links, load, store, send, recv,
 ):
     me = lax.axis_index("dom")
@@ -79,10 +79,18 @@
     def link(q, t):
         return jnp.clip(links[q, t], 0, TILES)
 
+    at_x, at_z, at_y = chip // 16, lax.rem(chip // 4, 4), lax.rem(chip, 4)
+
+    def moved(dx, dz, dy):
+        return (
+            lax.rem(at_x + dx, 4) * 16 + lax.rem(at_z + dz, 4) * 4 + lax.rem(at_y + dy, 4)
+        )
+
     def to_plane(source, target, slot):
         @pl.loop(1, CHIPS)
         def _(j):
-            there = lax.rem(chip + 23 * j, CHIPS)
+            step = lax.rem(j * 43, CHIPS)
+            there = moved(step // 16, lax.rem(step // 4, 4), lax.rem(step, 4))
             remote(source(there), target, slot, 2 * there + core).start()
 
     slot_iota = lax.broadcasted_iota(jnp.int32, (SLOTS, N), 0)
@@ -120,30 +128,36 @@
         )
         halo_out[block] = rows.reshape(32, SLOTS, F).astype(BF16)
 
-    def send_block(block, first):
-        @pl.loop(first, 32)
+    quarter = lax.rem(me, 4)
+
+    def block_of(b):
+        return 2 * lax.rem(at_y + b // 2, 2) + lax.rem(core + b, 2)
+
+    def send_block(b):
+        block = block_of(b)
+
+        @pl.loop(1 if b == 0 else 0, 32)
         def _(j):
-            there = lax.rem(me // 4 + 11 * j, 32)
-            remote(
-                halo_out.at[block, there], halo_in.at[me], HALO, 4 * there + block
-            ).start()
-
-    quarter = lax.rem(me, 4)
+            step = lax.rem(j * 11, 32)
+            there = moved(step // 8, lax.rem(step // 2, 4), 2 * lax.rem(step, 2) + b // 2)
+            peer = 2 * there + lax.rem(block, 2)
+            remote(halo_out.at[block, peer // 4], halo_in.at[me], HALO, peer).start()
+
     gather(quarter)
     pl.semaphore_wait(barrier, N - 1)
     pair = remote(hub_own.at[other], hub_got.at[0], PAIR, sibling)
     pair.start()
     pltpu.make_async_copy(halo_out.at[quarter, me // 4], halo_in.at[me], recv.at[HALO]).start()
-    send_block(quarter, 1)
-    gather(lax.rem(quarter + 1, 4))
+    send_block(0)
+    gather(block_of(1))
     pair.wait()
     hub_half[0] = hub_own[core] + hub_got[0]
     pltpu.make_async_copy(hub_half.at[0], hub_in.at[core, chip], recv.at[HUB]).start()
     to_plane(lambda there: hub_half.at[0], hub_in.at[core, chip], HUB)
-    send_block(lax.rem(quarter + 1, 4), 0)
+    send_block(1)
     for b in range(2, 4):
-        gather(lax.rem(quarter + b, 4))
-        send_block(lax.rem(quarter + b, 4), 0)
+        gather(block_of(b))
+        send_block(b)
 
     ids[...] = jnp.zeros_like(ids)
     ids[0:1, 0:TILES] = rows_ref[...]
@@ -209,48 +223,31 @@
             )
 
     loads[2].wait()
-    term[...] = jnp.zeros_like(term)
     weight = weight_ref[...]
 
-    @pl.loop(0, 4)
-    def _(k):
-        parts = [sums[link(0, TILES + 4 * k + j)] for j in range(4)]
-        agg = jnp.concatenate(parts, axis=0).astype(BF16)
-        pre = jnp.dot(agg, weight, preferred_element_type=F32)
-        sig = 0.5 * jnp.tanh(0.5 * pre) + 0.5
-        here = pl.ds(pl.multiple_of(k * 512, 512), 512)
-        out[here, :] = (pre * sig).astype(BF16)
-        gpre = (cot[here, :].astype(F32) * sig * (1.0 + pre * (1.0 - sig))).astype(BF16)
-        term[...] += transposed_dot(agg, gpre)
-        back = lax.dot_general(gpre, weight, (((1,), (1,)), ((), ())), preferred_element_type=F32)
-        gagg[pl.ds(4 * k, 4)] = back.astype(BF16).reshape(4, TILE, F)
+    agg = jnp.concatenate([sums[link(0, TILES + j)] for j in range(16)], axis=0).astype(BF16)
+    near[pl.ds(0, 16)] = agg.reshape(16, TILE, F)
+    pre = jnp.dot(agg, weight, preferred_element_type=F32)
+    sig = 0.5 * jnp.tanh(0.5 * pre) + 0.5
+    out[...] = (pre * sig).astype(BF16)
+    gpre = (cot[...].astype(F32) * sig * (1.0 + pre * (1.0 - sig))).astype(BF16)
+    cot[...] = gpre
+    back = lax.dot_general(gpre, weight, (((1,), (1,)), ((), ())), preferred_element_type=F32)
+    gagg[...] = back.astype(BF16).reshape(16, TILE, F)
 
     save_out = pltpu.make_async_copy(out, out_hbm, store.at[0])
     save_out.start()
-    whole = (term[...] * (1.0 / 512.0)).reshape(CHIPS, 8, F).astype(BF16)
-    term_out[0] = whole[:, :, :HALF]
-    term_out[1] = whole[:, :, HALF:]
-    pair = remote(term_out.at[other], term_got, TERM_PAIR, sibling)
-    pair.start()
 
     def spread_tile(t):
         sums[t + 1] = sums[link(1, t)] + transposed_dot(tiles[t], gagg[rows_s[t]])
 
-    @pl.loop(0, 16 // STEP)
-    def _(g):
-        for u in range(STEP):
-            spread_tile(NEAR + STEP * g + u)
-
-    pair.wait()
-    term_half[...] = (term_out[core].astype(F32) + term_got[...].astype(F32)).astype(BF16)
-    pltpu.make_async_copy(term_half.at[chip], term_in.at[chip], recv.at[TERM]).start()
-    to_plane(lambda there: term_half.at[there], term_in.at[chip], TERM)
-
-    @pl.loop(16 // STEP, (TILES - NEAR) // STEP)
-    def _(g):
-        for u in range(STEP):
-            spread_tile(NEAR + STEP * g + u)
-
+    def spread(first, last):
+        @pl.loop(first // STEP, last // STEP)
+        def _(g):
+            for u in range(STEP):
+                spread_tile(STEP * g + u)
+
+    spread(NEAR, TILES)
     for b in range(8):
         rows = sums[link(1, TILES + 20 + b)]
         back_out[pl.ds(16 * b, 16)] = rows.reshape(16, SLOTS, F).astype(BF16)
@@ -259,32 +256,48 @@
 
     @pl.loop(1, N)
     def _(i):
-        peer = lax.rem(me + 37 * i, N)
+        step = lax.rem(i * 91, N)
+        there = moved(step // 32, lax.rem(step // 8, 4), lax.rem(step // 2, 4))
+        peer = 2 * there + lax.rem(core + step, 2)
         remote(back_out.at[peer], landing, BACK, peer).start()
 
-    @pl.loop(0, NEAR // STEP)
-    def _(g):
-        for u in range(STEP):
-            spread_tile(STEP * g + u)
+    term[...] = jnp.zeros_like(term)
+
+    @pl.loop(0, 4)
+    def _(k):
+        here = pl.ds(pl.multiple_of(k * 512, 512), 512)
+        agg = near[pl.ds(4 * k, 4)].reshape(512, F)
+        term[...] += transposed_dot(agg, cot[here, :])
+
+    whole = (term[...] * (1.0 / 512.0)).reshape(CHIPS, 8, F).astype(BF16)
+    term_out[0] = whole[:, :, :HALF]
+    term_out[1] = whole[:, :, HALF:]
+    pair = remote(term_out.at[other], term_got, TERM_PAIR, sibling)
+    pair.start()
+    spread(0, 32)
+    pair.wait()
+    term_half[...] = (term_out[core].astype(F32) + term_got[...].astype(F32)).astype(BF16)
+    pltpu.make_async_copy(term_half.at[chip], term_in.at[chip], recv.at[TERM]).start()
+    to_plane(lambda there: term_half.at[there], term_in.at[chip], TERM)
+    spread(32, NEAR)
 
     for b in range(4):
         rows = sums[link(1, TILES + 16 + b)].reshape(16, 8, F).astype(BF16)
-        hub_out[0, pl.ds(16 * b, 16)] = rows[:, :, :HALF]
-        hub_out[1, pl.ds(16 * b, 16)] = rows[:, :, HALF:]
-    pair = remote(hub_out.at[other], hub_back_got, BACK_PAIR, sibling)
-    pair.start()
+        term_out[0, pl.ds(16 * b, 16)] = rows[:, :, :HALF]
+        term_out[1, pl.ds(16 * b, 16)] = rows[:, :, HALF:]
+    pair = remote(term_out.at[other], hub_back_got, BACK_PAIR, sibling)
+    pair.start()
+    pair.wait()
+    hub_back_half[...] = (
+        term_out[core].astype(F32) + hub_back_got[...].astype(F32)
+    ).astype(BF16)
+    pltpu.make_async_copy(hub_back_half.at[chip], hub_back.at[chip], recv.at[HUB_BACK]).start()
+    to_plane(lambda there: hub_back_half.at[there], hub_back.at[chip], HUB_BACK)
 
     whole_wait(term_in, recv.at[TERM])
     share[0] = jnp.sum(term_in[...].astype(F32), axis=0).astype(BF16)
     pltpu.make_async_copy(share.at[0], gathered.at[core, chip], recv.at[SHARE]).start()
     to_plane(lambda there: share.at[0], gathered.at[core, chip], SHARE)
-
-    pair.wait()
-    hub_back_half[...] = (
-        hub_out[core].astype(F32) + hub_back_got[...].astype(F32)
-    ).astype(BF16)
-    pltpu.make_async_copy(hub_back_half.at[chip], hub_back.at[chip], recv.at[HUB_BACK]).start()
-    to_plane(lambda there: hub_back_half.at[there], hub_back.at[chip], HUB_BACK)
 
     whole_wait(back_in, recv.at[BACK])
 
@@ -298,20 +311,13 @@
             at = link(1, TILES + 2 * k + j)
             sums[2 * k + j + MORE] = sums[at] + back[j * TILE : j * TILE + TILE]
 
-    whole_wait(gathered.at[core], recv.at[SHARE])
-    share_pair = remote(gathered.at[core], gathered.at[core], SHARE_PAIR, sibling)
-    share_pair.start()
-
     whole_wait(hub_back, recv.at[HUB_BACK])
     hub_pair[0] = jnp.sum(hub_back[...].astype(F32), axis=0)
     pair = remote(hub_pair.at[0], hub_pair.at[1], LAST_PAIR, sibling)
     pair.start()
+    hub_rows[...] = jnp.zeros_like(hub_rows)
     save_out.wait()
-    share_pair.wait()
-    save_weight = pltpu.make_async_copy(gathered, gweight_hbm, store.at[1])
-    save_weight.start()
-    pair.wait()
-    hub_rows[...] = jnp.zeros_like(hub_rows)
+    pair.wait()
     first = jnp.where(core == 0, hub_pair[0], hub_pair[1])
     second = jnp.where(core == 0, hub_pair[1], hub_pair[0])
     total = jnp.concatenate([first, second], axis=1)
@@ -327,6 +333,12 @@
 
     save_grad = pltpu.make_async_copy(out, gfeat_hbm, store.at[0])
     save_grad.start()
+    whole_wait(gathered.at[core], recv.at[SHARE])
+    pair = remote(gathered.at[core], gathered.at[core], SHARE_PAIR, sibling)
+    pair.start()
+    pair.wait()
+    save_weight = pltpu.make_async_copy(gathered, gweight_hbm, store.at[1])
+    save_weight.start()
     whole_wait(hub_back.at[pl.ds(0, CHIPS - 1)], send.at[HUB])
     whole_wait(halo_in.at[pl.ds(0, N - 1)], send.at[HALO])
     whole_wait(hub_back.at[pl.ds(0, CHIPS - 1)], send.at[TERM])
@@ -337,18 +349,34 @@
     save_weight.wait()
 
 
-def finish(out_in, gfeat_in, gathered_ref, out_ref, gfeat_ref, gweight_ref, sems):
-    copies = []
+def finish(
+    out_in, gfeat_in, gathered_hbm, out_ref, gfeat_ref, gweight_hbm, staged, gathered, gweight, come, go
+):
+    last = (
+        pltpu.make_async_copy(gathered_hbm, gathered, come.at[8]),
+        pltpu.make_async_copy(gweight, gweight_hbm, go.at[8]),
+    )
+    last[0].start()
+    pairs = []
     for a, (src, dst) in enumerate(((out_in, out_ref), (gfeat_in, gfeat_ref))):
         for b in range(4):
-            here = pl.ds(b * 512, 512)
-            copies.append(pltpu.make_async_copy(src.at[here], dst.at[here], sems.at[4 * a + b]))
-    for copy in copies:
-        copy.start()
+            here, slot = pl.ds(b * 512, 512), 4 * a + b
+            pairs.append((
+                pltpu.make_async_copy(src.at[here], staged.at[slot], come.at[slot]),
+                pltpu.make_async_copy(staged.at[slot], dst.at[here], go.at[slot]),
+            ))
+    for first, _ in pairs:
+        first.start()
+    last[0].wait()
     for q in range(2):
-        gweight_ref[:, :, q * HALF : q * HALF + HALF] = gathered_ref[q].astype(F32)
-    for copy in copies:
-        copy.wait()
+        gweight[:, :, q * HALF : q * HALF + HALF] = gathered[q].astype(F32)
+    last[1].start()
+    for first, second in pairs:
+        first.wait()
+        second.start()
+    for _, second in pairs:
+        second.wait()
+    last[1].wait()
 
 
 def per_device(
@@ -396,7 +424,6 @@
             pltpu.VMEM(plane, BF16),
             pltpu.VMEM((N, SLOTS, F), BF16),
             pltpu.VMEM((4, 32, SLOTS, F), BF16),
-            pltpu.VMEM(plane, BF16),
             pltpu.VMEM(plane[1:], BF16),
             pltpu.VMEM(plane[1:], BF16),
             pltpu.VMEM(plane[1:], BF16),
@@ -423,9 +450,15 @@
             jax.ShapeDtypeStruct((R, F), BF16),
             jax.ShapeDtypeStruct((CHIPS, 8, F), F32),
         ),
-        in_specs=[anywhere, anywhere, vmem],
-        out_specs=(anywhere, anywhere, vmem),
-        scratch_shapes=[pltpu.SemaphoreType.DMA((8,))],
+        in_specs=[anywhere] * 3,
+        out_specs=(anywhere,) * 3,
+        scratch_shapes=[
+            pltpu.VMEM((8, 512, F), BF16),
+            pltpu.VMEM(plane, BF16),
+            pltpu.VMEM((CHIPS, 8, F), F32),
+            pltpu.SemaphoreType.DMA((9,)),
+            pltpu.SemaphoreType.DMA((9,)),
+        ],
         name="finish",
     )(output, grad_features, gathered)
     return output, grad_features, grad_weight.reshape(F, F)

time: 200 us -> 72.2 us (0.36)
  Pallas kernels: 199 us -> 71.4 us
    pallas_call x1, Pallas kernels: 130 us -> 3.97 us  [per_device(): pl.pallas_call(finish, out_shape=(jax.ShapeDtypeStruct((R, F), BF16), jax...]
where the time goes in v4:
time: 72.2 us; the launch traced here: 72.1 us
  Pallas kernels  71.4 us (99%)
    pallas_call x1, Pallas kernels, per_device(): pl.pallas_call(body, out_shape=(jax.ShapeDtypeStruct((R, F), BF16), jax.S...  67.5 us
    pallas_call x1, Pallas kernels, per_device(): pl.pallas_call(finish, out_shape=(jax.ShapeDtypeStruct((R, F), BF16), jax...  3.97 us

profile of v4, /device:TPU:1, one launch (start us, length us, event | category | flops | bytes accessed | tf_op | source)
XLA Modules:
  0.0 72.1 jit_solution(6969448930890902898)
XLA Ops:
  0.6 67.5 %graph_layer.1 = (bf16[2048,512]{1,0:T(8,128)(2,1)}, bf16[2048,512]{1,0:T(8,128)(2,1)}, bf16[2,64,8,256]{3,2,1,0:T(8,128)(2,1)}) custom-call(s32[96]{0:T(128)} %rows_s.1, s32[96]{0:T(128)} %cols_s.1, s32[4]{0:T(128)} %hub_s.1, s32[1,96]{1,0:T(1,128)} %bitcast.9, s32[1,96]{1,0:T(1,128)} %bitcast.10, s32[8,128]{1,0:T(8,128)} %bitcast.8, s32[1,128]{1,0:T(1,128)} %count_ref.1, ...), custom_call_target="tpu_custom_call" | custom-call | tf_op jit(solution)/shard_map/graph_layer/pallas_call | solution.py:389
  68.1 4.0 %finish.1 = (bf16[2048,512]{1,0:T(8,128)(2,1)}, bf16[2048,512]{1,0:T(8,128)(2,1)}, f32[64,8,512]{2,1,0:T(8,128)}) custom-call(bf16[2048,512]{1,0:T(8,128)(2,1)} %get-tuple-element.9.out_in, bf16[2048,512]{1,0:T(8,128)(2,1)} %get-tuple-element.10.gfeat_in, bf16[2,64,8,256]{3,2,1,0:T(8,128)(2,1)} %get-tuple-element.11.gathered_hbm), custom_call_target="tpu_custom_call" | custom-call | tf_op jit(solution)/shard_map/finish/pallas_call | solution.py:446

commit v5 on v4

--- a/solution.py
+++ b/solution.py
@@ -247,7 +247,24 @@
             for u in range(STEP):
                 spread_tile(STEP * g + u)
 
+    term[...] = jnp.zeros_like(term)
+
+    @pl.loop(0, 4)
+    def _(k):
+        here = pl.ds(pl.multiple_of(k * 512, 512), 512)
+        agg = near[pl.ds(4 * k, 4)].reshape(512, F)
+        term[...] += transposed_dot(agg, cot[here, :])
+
+    whole = (term[...] * (1.0 / 512.0)).reshape(CHIPS, 8, F).astype(BF16)
+    term_out[0] = whole[:, :, :HALF]
+    term_out[1] = whole[:, :, HALF:]
+    pair = remote(term_out.at[other], term_got, TERM_PAIR, sibling)
+    pair.start()
     spread(NEAR, TILES)
+    pair.wait()
+    term_half[...] = (term_out[core].astype(F32) + term_got[...].astype(F32)).astype(BF16)
+    pltpu.make_async_copy(term_half.at[chip], term_in.at[chip], recv.at[TERM]).start()
+    to_plane(lambda there: term_half.at[there], term_in.at[chip], TERM)
     for b in range(8):
         rows = sums[link(1, TILES + 20 + b)]
         back_out[pl.ds(16 * b, 16)] = rows.reshape(16, SLOTS, F).astype(BF16)
@@ -256,29 +273,10 @@
 
     @pl.loop(1, N)
     def _(i):
-        step = lax.rem(i * 91, N)
-        there = moved(step // 32, lax.rem(step // 8, 4), lax.rem(step // 2, 4))
-        peer = 2 * there + lax.rem(core + step, 2)
+        peer = lax.rem(me + 37 * i, N)
         remote(back_out.at[peer], landing, BACK, peer).start()
 
-    term[...] = jnp.zeros_like(term)
-
-    @pl.loop(0, 4)
-    def _(k):
-        here = pl.ds(pl.multiple_of(k * 512, 512), 512)
-        agg = near[pl.ds(4 * k, 4)].reshape(512, F)
-        term[...] += transposed_dot(agg, cot[here, :])
-
-    whole = (term[...] * (1.0 / 512.0)).reshape(CHIPS, 8, F).astype(BF16)
-    term_out[0] = whole[:, :, :HALF]
-    term_out[1] = whole[:, :, HALF:]
-    pair = remote(term_out.at[other], term_got, TERM_PAIR, sibling)
-    pair.start()
     spread(0, 32)
-    pair.wait()
-    term_half[...] = (term_out[core].astype(F32) + term_got[...].astype(F32)).astype(BF16)
-    pltpu.make_async_copy(term_half.at[chip], term_in.at[chip], recv.at[TERM]).start()
-    to_plane(lambda there: term_half.at[there], term_in.at[chip], TERM)
     spread(32, NEAR)
 
     for b in range(4):
@@ -324,15 +322,15 @@
     upper = total.astype(BF16).astype(F32)
     hub_rows[pl.ds(0, 16), :] = jnp.concatenate([upper, total - upper], axis=0).astype(BF16)
 
-    @pl.loop(0, 8)
-    def _(k):
-        here = pl.ds(pl.multiple_of(k * HALF, HALF), HALF)
+    saves = []
+    for k in range(4):
+        here = pl.ds(k * 512, 512)
         hub = jnp.dot(hub_picks[here, :], hub_rows[...], preferred_element_type=F32)
-        mine = sums[pl.ds(2 * k + MORE, 2)].reshape(HALF, F)
+        mine = sums[pl.ds(4 * k + MORE, 4)].reshape(512, F)
         out[here, :] = (mine + hub).astype(BF16)
-
-    save_grad = pltpu.make_async_copy(out, gfeat_hbm, store.at[0])
-    save_grad.start()
+        saves.append(pltpu.make_async_copy(out.at[here], gfeat_hbm.at[here], store.at[2 + k]))
+        saves[k].start()
+
     whole_wait(gathered.at[core], recv.at[SHARE])
     pair = remote(gathered.at[core], gathered.at[core], SHARE_PAIR, sibling)
     pair.start()
@@ -345,7 +343,8 @@
     whole_wait(halo_in.at[pl.ds(0, N - 1)], send.at[BACK])
     whole_wait(hub_back.at[pl.ds(0, CHIPS - 1)], send.at[HUB_BACK])
     whole_wait(hub_back.at[pl.ds(0, CHIPS - 1)], send.at[SHARE])
-    save_grad.wait()
+    for copy in saves:
+        copy.wait()
     save_weight.wait()
 
 
@@ -431,7 +430,7 @@
             pltpu.VMEM((TILE, F), BF16),
             pltpu.SMEM((8, TILE), jnp.int32),
             pltpu.SemaphoreType.DMA((4,)),
-            pltpu.SemaphoreType.DMA((2,)),
+            pltpu.SemaphoreType.DMA((6,)),
             pltpu.SemaphoreType.DMA((12,)),
             pltpu.SemaphoreType.DMA((12,)),
         ],

time: 72.2 us -> 71.3 us (0.988)
  Pallas kernels: 71.4 us -> 70.6 us
    pallas_call x1, Pallas kernels: 67.5 us -> 66.6 us  [per_device(): pl.pallas_call(body, out_shape=(jax.ShapeDtypeStruct((R, F), BF16), jax.S...]
where the time goes in v5:
time: 71.3 us; the launch traced here: 71.2 us
  Pallas kernels  70.6 us (99%)
    pallas_call x1, Pallas kernels, per_device(): pl.pallas_call(body, out_shape=(jax.ShapeDtypeStruct((R, F), BF16), jax.S...  66.6 us
    pallas_call x1, Pallas kernels, per_device(): pl.pallas_call(finish, out_shape=(jax.ShapeDtypeStruct((R, F), BF16), jax...  3.97 us

profile of v5, /device:TPU:1, one launch (start us, length us, event | category | flops | bytes accessed | tf_op | source)
XLA Modules:
  0.0 71.2 jit_solution(9877024096176368025)
XLA Ops:
  0.6 66.6 %graph_layer.1 = (bf16[2048,512]{1,0:T(8,128)(2,1)}, bf16[2048,512]{1,0:T(8,128)(2,1)}, bf16[2,64,8,256]{3,2,1,0:T(8,128)(2,1)}) custom-call(s32[96]{0:T(128)} %rows_s.1, s32[96]{0:T(128)} %cols_s.1, s32[4]{0:T(128)} %hub_s.1, s32[1,96]{1,0:T(1,128)} %bitcast.9, s32[1,96]{1,0:T(1,128)} %bitcast.10, s32[8,128]{1,0:T(8,128)} %bitcast.8, s32[1,128]{1,0:T(1,128)} %count_ref.1, ...), custom_call_target="tpu_custom_call" | custom-call | tf_op jit(solution)/shard_map/graph_layer/pallas_call | solution.py:388
  67.2 4.0 %finish.1 = (bf16[2048,512]{1,0:T(8,128)(2,1)}, bf16[2048,512]{1,0:T(8,128)(2,1)}, f32[64,8,512]{2,1,0:T(8,128)}) custom-call(bf16[2048,512]{1,0:T(8,128)(2,1)} %get-tuple-element.9.out_in, bf16[2048,512]{1,0:T(8,128)(2,1)} %get-tuple-element.10.gfeat_in, bf16[2,64,8,256]{3,2,1,0:T(8,128)(2,1)} %get-tuple-element.11.gathered_hbm), custom_call_target="tpu_custom_call" | custom-call | tf_op jit(solution)/shard_map/finish/pallas_call | solution.py:445
